TPU v7x, 32 devices: a whole 2x2x4 slice. The times are simulated.
32 devices in a mesh: wshard: 8 (over z, y), seq: 4 (over x, core).
Axes of the slice: x: 2, y: 2, z: 4, core: 2. Of those that a mesh axis runs over, the one named last changes fastest.
Arguments:
- tokens: bfloat16 [24576, 768], P(('wshard', 'seq')), may hold values from -6 to 6
- cotangent: bfloat16 [24576, 768], P(('wshard', 'seq')), may hold values from -6 to 6
- starts: int32 [8, 8], P('wshard'), may hold values from 0 to 2688, as said below
- w_query: bfloat16 [768, 768], P('wshard'), may hold values from -0.21875 to 0.21875
- w_key: bfloat16 [768, 768], P('wshard'), may hold values from -0.21875 to 0.21875
- w_value: bfloat16 [768, 768], P('wshard'), may hold values from -0.21875 to 0.21875
- w_output: bfloat16 [768, 768], P('wshard'), may hold values from -1.25 to 1.25
- w_inner: bfloat16 [768, 3072], P('wshard'), may hold values from -0.21875 to 0.21875
- w_outer: bfloat16 [3072, 768], P('wshard'), may hold values from -0.109375 to 0.109375
- b_query: bfloat16 [768], P('wshard'), may hold values from -3 to 3
- b_value: bfloat16 [768], P('wshard'), may hold values from -3 to 3
- b_output: bfloat16 [768], P('wshard'), may hold values from -3 to 3
- b_inner: bfloat16 [3072], P('wshard'), may hold values from -3 to 3
- b_outer: bfloat16 [768], P('wshard'), may hold values from -3 to 3
- gain_first: bfloat16 [768], P('wshard'), may hold values from 0.5 to 2
- bias_first: bfloat16 [768], P('wshard'), may hold values from -3 to 3
- gain_second: bfloat16 [768], P('wshard'), may hold values from 0.5 to 2
- bias_second: bfloat16 [768], P('wshard'), may hold values from -3 to 3
Outputs:
- layer_out: bfloat16 [24576, 768], P(('wshard', 'seq'))
- grad_tokens: float32 [24576, 768], P(('wshard', 'seq'))
- grad_w_query: float32 [768, 768], P('wshard')
- grad_w_key: float32 [768, 768], P('wshard')
- grad_w_value: float32 [768, 768], P('wshard')
- grad_w_output: float32 [768, 768], P('wshard')
- grad_w_inner: float32 [768, 3072], P('wshard')
- grad_w_outer: float32 [3072, 768], P('wshard')
- grad_b_query: float32 [768], P('wshard')
- grad_b_value: float32 [768], P('wshard')
- grad_b_output: float32 [768], P('wshard')
- grad_b_inner: float32 [3072], P('wshard')
- grad_b_outer: float32 [768], P('wshard')
- grad_gain_first: float32 [768], P('wshard')
- grad_bias_first: float32 [768], P('wshard')
- grad_gain_second: float32 [768], P('wshard')
- grad_bias_second: float32 [768], P('wshard')
Inputs may be any that keep to these rules, and one draw needn't show every extreme that they name: `starts`: row w lists where the 8 documents of stream w begin: the first is 0 and they strictly increase; the last document of every stream holds exactly 384 positions; documents run across the devices of a stream.
All inputs are finite; a program needn't handle non-finite values.
Results may differ from a plain program's by a relative error of at most 0.017.
Values may be sent and summed in bfloat16 or wider, within the bound.
A program may use at most 192 MiB of HBM per device.

v0:
```python
import functools

import jax
import jax.numpy as jnp
from jax import lax
from jax.experimental import pallas as pl
from jax.experimental.pallas import tpu as pltpu
from jax.sharding import PartitionSpec as P

NORM_EPS = 1e-05
HD = 64
bf = jnp.bfloat16
f32 = jnp.float32


def doc_bounds(starts_ref, pos, total):
    lo = jnp.zeros_like(pos); hi = jnp.full_like(pos, total)
    for d in range(starts_ref.shape[1]):
        s = starts_ref[0, d]
        lo = jnp.where(s <= pos, jnp.maximum(lo, s), lo)
        hi = jnp.where(s > pos, jnp.minimum(hi, s), hi)
    return lo, hi

def dot(a, b):
    return lax.dot_general(a, b, (((1,), (0,)), ((), ())), preferred_element_type=f32)

def dot_first(a, b):
    return lax.dot_general(a, b, (((0,), (0,)), ((), ())), preferred_element_type=f32)

def turned(a):
    return a.astype(f32).T.astype(bf)

def fwd_kernel(heads, bq, bk, starts, qT, kT, vT, oT, mix, lse, acc, ml):
    total = kT.shape[1]
    toks = mix.shape[2]
    i = pl.program_id(0)
    q0 = i * bq
    first, _ = doc_bounds(starts, jnp.int32(q0), total)
    _, last = doc_bounds(starts, jnp.int32(q0 + bq - 1), total)
    pos = q0 + lax.broadcasted_iota(jnp.int32, (1, bq), 1)
    lo, hi = doc_bounds(starts, pos, total)
    kb0 = first // bk
    kb1 = (last + bk - 1) // bk
    acc[...] = jnp.zeros_like(acc)
    ml[0] = jnp.full((heads, bq), -1e30, f32)
    ml[1] = jnp.zeros((heads, bq), f32)
    kio = lax.broadcasted_iota(jnp.int32, (bk, bq), 0)
    def body(j, _):
        ks = pl.multiple_of(j * bk, bk)
        mask = (kio >= lo - ks) & (kio < hi - ks)
        for h in range(heads):
            sl = slice(HD * h, HD * (h + 1))
            s = dot_first(kT[sl, pl.ds(ks, bk)], qT[sl, :])
            s = jnp.where(mask, s, -1e30)
            m_old = ml[0, h:h + 1]
            m = jnp.maximum(m_old, jnp.max(s, axis=0, keepdims=True))
            p = jnp.exp(s - m)
            al = jnp.exp(m_old - m)
            ml[0, h:h + 1] = m
            ml[1, h:h + 1] = ml[1, h:h + 1] * al + jnp.sum(p, axis=0, keepdims=True)
            acc[sl, :] = acc[sl, :] * al + dot(vT[sl, pl.ds(ks, bk)], p.astype(bf))
        return 0
    lax.fori_loop(kb0, kb1, body, 0)
    step = min(bq, 256)
    for h in range(heads):
        sl = slice(HD * h, HD * (h + 1))
        l = ml[1, h:h + 1]
        o = acc[sl, :] / l
        oT[sl, :] = o
        for t in range(0, bq, step):
            at = q0 + t
            mix[at // toks, sl, pl.ds(pl.multiple_of(at % toks, step), step)] = o[:, t:t + step].astype(bf)
        lse[h:h + 1, :] = ml[0, h:h + 1] + jnp.log(l)

def attn_fwd(starts, qkv, toks, bq, bk):
    width, total = qkv.shape[0] // 3, qkv.shape[1]
    heads = width // HD
    return pl.pallas_call(
        functools.partial(fwd_kernel, heads, bq, bk),
        grid=(total // bq,),
        in_specs=[pl.BlockSpec(memory_space=pltpu.SMEM),
                  pl.BlockSpec((width, bq), lambda i: (0, i)),
                  pl.BlockSpec((width, total), lambda i: (1, 0)),
                  pl.BlockSpec((width, total), lambda i: (2, 0))],
        out_specs=[pl.BlockSpec((width, bq), lambda i: (0, i)),
                   pl.BlockSpec((total // toks, width, toks), lambda i: (0, 0, 0)),
                   pl.BlockSpec((heads, bq), lambda i: (0, i))],
        out_shape=[jax.ShapeDtypeStruct((width, total), f32),
                   jax.ShapeDtypeStruct((total // toks, width, toks), bf),
                   jax.ShapeDtypeStruct((heads, total), f32)],
        scratch_shapes=[pltpu.VMEM((width, bq), f32), pltpu.VMEM((2, heads, bq), f32)],
        cost_estimate=pl.CostEstimate(flops=8 * width * total * total, bytes_accessed=8 * width * total, transcendentals=0),
        name="attn_fwd",
    )(starts, qkv, qkv, qkv)

def bwd_kernel(heads, bq, bk, starts, qT, kT, vT, doT, oT, lse, dT, q3, do3, delta, dqa, dka, dva):
    width, total = qT.shape
    toks = doT.shape[2]
    i = pl.program_id(0)
    k0 = pl.multiple_of(i * bk, bk)
    @pl.when(i == 0)
    def _():
        dqa[...] = jnp.zeros_like(dqa)
        for h in range(heads):
            sl = slice(HD * h, HD * (h + 1))
            for b in range(doT.shape[0]):
                at = slice(b * toks, (b + 1) * toks)
                delta[h:h + 1, at] = jnp.sum(doT[b, sl, :].astype(f32) * oT[sl, at], axis=0, keepdims=True)
                q3[h, at, :] = turned(qT[sl, at])
                do3[h, at, :] = turned(doT[b, sl, :])
    first, _ = doc_bounds(starts, jnp.int32(k0), total)
    _, last = doc_bounds(starts, jnp.int32(k0 + bk - 1), total)
    qb0 = first // bq
    qb1 = (last + bq - 1) // bq
    dka[...] = jnp.zeros_like(dka)
    dva[...] = jnp.zeros_like(dva)
    kio = k0 + lax.broadcasted_iota(jnp.int32, (bk, bq), 0)
    def body(j, _):
        qs = pl.multiple_of(j * bq, bq)
        pos = qs + lax.broadcasted_iota(jnp.int32, (1, bq), 1)
        lo, hi = doc_bounds(starts, pos, total)
        mask = (kio >= lo) & (kio < hi)
        for h in range(heads):
            sl = slice(HD * h, HD * (h + 1))
            s = dot_first(kT[sl, :], qT[sl, pl.ds(qs, bq)])
            p = jnp.exp(jnp.where(mask, s - lse[h:h + 1, pl.ds(qs, bq)], -1e30))
            dp = dot_first(vT[sl, :], doT[qs // toks, sl, pl.ds(pl.multiple_of(qs % toks, bq), bq)])
            ds = p * (dp - delta[h:h + 1, pl.ds(qs, bq)])
            dsb = ds.astype(bf)
            dva[h] += dot(p.astype(bf), do3[h, pl.ds(qs, bq), :])
            dka[h] += dot(dsb, q3[h, pl.ds(qs, bq), :])
            dqa[sl, pl.ds(qs, bq)] += dot(kT[sl, :], dsb)
        return 0
    lax.fori_loop(qb0, qb1, body, 0)
    for h in range(heads):
        dT[width + HD * h:width + HD * (h + 1), pl.ds(k0, bk)] = dka[h].T.astype(bf)
        dT[2 * width + HD * h:2 * width + HD * (h + 1), pl.ds(k0, bk)] = dva[h].T.astype(bf)
    @pl.when(i == pl.num_programs(0) - 1)
    def _():
        dT[0:width, :] = (dqa[...] * (HD ** -0.5)).astype(bf)

def attn_bwd(starts, qkv, doT, oT, lse, bq, bk):
    width, total = qkv.shape[0] // 3, qkv.shape[1]
    heads = width // HD
    full = lambda a: pl.BlockSpec(a.shape, lambda i: (0,) * a.ndim)
    return pl.pallas_call(
        functools.partial(bwd_kernel, heads, bq, bk),
        grid=(total // bk,),
        in_specs=[pl.BlockSpec(memory_space=pltpu.SMEM),
                  pl.BlockSpec((width, total), lambda i: (0, 0)), pl.BlockSpec((width, bk), lambda i: (1, i)),
                  pl.BlockSpec((width, bk), lambda i: (2, i)), full(doT), full(oT), full(lse)],
        out_specs=pl.BlockSpec(qkv.shape, lambda i: (0, 0)),
        out_shape=jax.ShapeDtypeStruct(qkv.shape, bf),
        scratch_shapes=[pltpu.VMEM((heads, total, HD), bf), pltpu.VMEM((heads, total, HD), bf),
                        pltpu.VMEM((heads, total), f32), pltpu.VMEM((width, total), f32),
                        pltpu.VMEM((heads, bk, HD), f32), pltpu.VMEM((heads, bk, HD), f32)],
        cost_estimate=pl.CostEstimate(flops=8 * width * total * total, bytes_accessed=8 * width * total, transcendentals=0),
        name="attn_bwd",
    )(starts, qkv, qkv, qkv, doT, oT, lse)


MESH = pl.DeviceIdType.MESH


class Wire:
    def __init__(self, send, recv):
        self.send, self.recv, self.used, self.open = send, recv, 0, []

    def slot(self):
        self.used += 1
        return self.used - 1

    def start(self, slot, src, dst, device):
        copy = pltpu.make_async_remote_copy(
            src_ref=src, dst_ref=dst, send_sem=self.send.at[slot], recv_sem=self.recv.at[slot],
            device_id=device, device_id_type=MESH,
        )
        copy.start()
        self.open.append(copy)
        return copy

    def arrived(self, slot, dst, device):
        pltpu.make_async_remote_copy(
            src_ref=dst, dst_ref=dst, send_sem=self.send.at[slot], recv_sem=self.recv.at[slot],
            device_id=device, device_id_type=MESH,
        ).wait_recv()

    def sent(self, copy):
        copy.wait_send()
        self.open = [other for other in self.open if other is not copy]

    def drain(self):
        for copy in self.open:
            copy.wait_send()
        self.open = []


def grid_peers():
    shard, seq = lax.axis_index("wshard"), lax.axis_index("seq")
    z, y = shard // 2, shard % 2
    x, c = seq // 2, seq % 2
    at = lambda zz, yy, xx, cc: (zz * 2 + yy, xx * 2 + cc)
    along = [at((z + d) % 4, y, x, c) for d in range(4)]
    return z, y, x, c, along, at(z, 1 - y, x, c), at(z, y, 1 - x, c), at(z, y, x, 1 - c)


def greet(peers):
    barrier = pltpu.get_barrier_semaphore()
    for peer in peers:
        pl.semaphore_signal(barrier, inc=1, device_id=peer, device_id_type=MESH)
    pl.semaphore_wait(barrier, len(peers))


ORDER = (1, 3, 2)


def gather_kernel(b_ref, t_ref, q_ref, x_ref, send, recv, lsem):
    z, y, x, c, along, ypeer, xpeer, cpeer = grid_peers()
    own = z * 2 + y
    wire = Wire(send, recv)
    spot = lambda r, d: ((z + 4 - d) % 4) * 2 + (y if r == 0 else 1 - y)
    seq = x * 2 + c
    half = t_ref.shape[0] // 2
    parts = [pl.ds(0, half), pl.ds(half, half)]
    locals_ = [
        pltpu.make_async_copy(b_ref, q_ref.at[own], lsem.at[0]),
        pltpu.make_async_copy(t_ref, x_ref.at[seq], lsem.at[1]),
    ]
    for copy in locals_:
        copy.start()
    greet(along[1:] + [ypeer, xpeer, cpeer])
    zB = [wire.slot() for _ in range(4)]
    yB = [wire.slot() for _ in range(4)]
    tx, tc1 = [wire.slot() for _ in parts], [wire.slot() for _ in parts]
    tc0 = wire.slot()
    for slot, part in zip(tx, parts):
        wire.start(slot, t_ref.at[part], x_ref.at[seq, part], xpeer)
    for d in ORDER:
        wire.start(zB[d], b_ref, q_ref.at[own], along[d])
    wire.start(yB[0], b_ref, q_ref.at[own], ypeer)
    wire.start(tc0, t_ref, x_ref.at[seq], cpeer)
    for d in ORDER:
        w = spot(0, d)
        wire.arrived(zB[d], q_ref.at[w], along[d])
        wire.start(yB[d], q_ref.at[w], q_ref.at[w], ypeer)
    xtok = (1 - x) * 2 + c
    for i, part in enumerate(parts):
        wire.arrived(tx[i], x_ref.at[xtok, part], xpeer)
        wire.start(tc1[i], x_ref.at[xtok, part], x_ref.at[xtok, part], cpeer)
    for d in (0,) + ORDER:
        wire.arrived(yB[d], q_ref.at[spot(1, d)], ypeer)
    wire.arrived(tc0, x_ref.at[x * 2 + 1 - c], cpeer)
    for i, part in enumerate(parts):
        wire.arrived(tc1[i], x_ref.at[(1 - x) * 2 + 1 - c, part], cpeer)
    wire.drain()
    for copy in locals_:
        copy.wait()


def gather_inputs(b, tokens):
    slots = 13
    hbm = pl.BlockSpec(memory_space=pl.ANY)
    vmem = pl.BlockSpec(memory_space=pltpu.VMEM)
    return pl.pallas_call(
        gather_kernel,
        in_specs=[vmem] * 2, out_specs=[hbm] * 2,
        out_shape=[jax.ShapeDtypeStruct((8,) + b.shape, b.dtype), jax.ShapeDtypeStruct((4,) + tokens.shape, tokens.dtype)],
        scratch_shapes=[pltpu.SemaphoreType.DMA((slots,)), pltpu.SemaphoreType.DMA((slots,)), pltpu.SemaphoreType.DMA((2,))],
        compiler_params=pltpu.CompilerParams(collective_id=1, has_side_effects=True),
        name="gather_inputs",
    )(b, tokens)


def add_rows(dst, parts, rows, step=16):
    def body(i, _):
        at = pl.ds(pl.multiple_of(i * step, step), step)
        total = parts[0][at, :].astype(f32)
        for part in parts[1:]:
            total = total + part[at, :].astype(f32)
        dst[at, :] = total.astype(dst.dtype)
        return 0
    lax.fori_loop(0, rows // step, body, 0)


ALL = ORDER + (0,)


def reduce_kernel(ga, gb, dx, sm, fa, fb, fx, fr, fs, hb, ryb, rzb, rxc, hs, rys, rzs, s1, s2, s3, s4, rg, send, recv):
    z, y, x, c, along, ypeer, xpeer, cpeer = grid_peers()
    wire = Wire(send, recv)
    new = lambda count: [wire.slot() for _ in range(count)]
    kc, kx, kg, kyb, kys = new(4), new(2), new(2), wire.slot(), wire.slot()
    kzb, kzs, fin = new(4), new(4), new(8)
    zz = lambda d: (z + d) % 4
    half = dx.shape[2] // 2
    halves = [pl.ds(0, half), pl.ds(half, half)]
    sizes = [ga.shape[0] // 32 * 16, ga.shape[0] - ga.shape[0] // 32 * 16]
    pieces = [pl.ds(0, sizes[0]), pl.ds(sizes[0], sizes[1])]
    greet(along[1:] + [ypeer, xpeer, cpeer])
    for i, at in enumerate(halves):
        wire.start(kc[i], dx.at[1 - x, 1 - c, at], rxc.at[1 - x, at], cpeer)
    wire.start(kg[0], ga.at[pieces[0]], rg.at[pieces[0]], xpeer)
    wire.start(kys, sm.at[:, 1 - y], rys, ypeer)
    wire.start(kyb, gb.at[:, 1 - y], ryb, ypeer)
    for i, at in enumerate(halves):
        wire.start(kc[2 + i], dx.at[x, 1 - c, at], rxc.at[x, at], cpeer)
    for i, at in enumerate(halves):
        spot = rxc.at[1 - x, at]
        wire.arrived(kc[i], spot, cpeer)
        add_rows(spot, [dx.at[1 - x, c, at], spot], half)
        wire.start(kx[i], spot, fr.at[at], xpeer)
    wire.start(kg[1], ga.at[pieces[1]], rg.at[pieces[1]], xpeer)
    wire.arrived(kys, rys, ypeer)
    wire.arrived(kyb, ryb, ypeer)
    for d in ALL:
        hs[d] = sm[zz(d), y] + rys[zz(d)]
        add_rows(hb.at[d], [gb.at[zz(d), y], ryb.at[zz(d)]], hb.shape[1])
        if d:
            wire.start(kzs[d], hs.at[d], rzs.at[d], along[d])
            wire.start(kzb[d], hb.at[d], rzb.at[d], along[d])
    for i, at in enumerate(halves):
        wire.arrived(kc[2 + i], rxc.at[x, at], cpeer)
        add_rows(fx.at[at], [dx.at[x, c, at], rxc.at[x, at]], half)
    wire.arrived(kg[0], rg.at[pieces[0]], xpeer)
    add_rows(fa.at[c, pieces[0]], [ga.at[pieces[0]], rg.at[pieces[0]]], sizes[0])
    wire.start(fin[5], fa.at[c, pieces[0]], fa.at[c, pieces[0]], cpeer)
    for d in ORDER:
        wire.arrived(kzs[d], rzs.at[d], along[d])
        wire.arrived(kzb[d], rzb.at[d], along[d])
    s1[...] = hs[0] + rzs[1] + rzs[2] + rzs[3]
    wire.start(fin[0], s1, s2, xpeer)
    seq, xseq = 2 * x + c, 2 * (1 - x) + c
    add_rows(fb.at[seq], [hb.at[0]] + [rzb.at[d] for d in ORDER], hb.shape[1])
    wire.start(fin[1], fb.at[seq], fb.at[seq], xpeer)
    wire.start(fin[2], fb.at[seq], fb.at[seq], cpeer)
    for i, at in enumerate(halves):
        wire.arrived(kx[i], fr.at[at], xpeer)
    wire.arrived(kg[1], rg.at[pieces[1]], xpeer)
    add_rows(fa.at[c, pieces[1]], [ga.at[pieces[1]], rg.at[pieces[1]]], sizes[1])
    wire.start(fin[6], fa.at[c, pieces[1]], fa.at[c, pieces[1]], cpeer)
    wire.arrived(fin[0], s2, xpeer)
    s3[...] = s1[...] + s2[...]
    wire.start(fin[3], s3, s4, cpeer)
    wire.arrived(fin[1], fb.at[xseq], xpeer)
    wire.start(fin[4], fb.at[xseq], fb.at[xseq], cpeer)
    wire.arrived(fin[3], s4, cpeer)
    fs[...] = s3[...] + s4[...]
    wire.arrived(fin[2], fb.at[2 * x + 1 - c], cpeer)
    wire.arrived(fin[4], fb.at[2 * (1 - x) + 1 - c], cpeer)
    for i in range(2):
        wire.arrived(fin[5 + i], fa.at[1 - c, pieces[i]], cpeer)
    wire.drain()


def reduce_grads(ga, gb, dx, sm):
    rows, cols = ga.shape
    toks = dx.shape[1]
    vmem = pl.BlockSpec(memory_space=pltpu.VMEM)
    b0, b1 = gb.shape[1:]
    V = pltpu.VMEM
    sv = lambda *lead: V(lead + sm.shape[1:], f32)
    slots = 26
    return pl.pallas_call(
        reduce_kernel,
        in_specs=[vmem] * 4, out_specs=[vmem] * 5,
        out_shape=[jax.ShapeDtypeStruct((2, rows, cols), bf), jax.ShapeDtypeStruct((4, b0, b1), bf),
                   jax.ShapeDtypeStruct((toks, cols), bf), jax.ShapeDtypeStruct((toks, cols), bf),
                   jax.ShapeDtypeStruct(sm.shape[1:], f32)],
        scratch_shapes=[V((4, b0, b1), bf), V((4, b0, b1), bf), V((4, b0, b1), bf), V((2, toks, cols), bf),
                        sv(4), sv(4), sv(4), sv(), sv(), sv(), sv(), V((rows, cols), bf),
                        pltpu.SemaphoreType.DMA((slots,)), pltpu.SemaphoreType.DMA((slots,))],
        compiler_params=pltpu.CompilerParams(collective_id=2, has_side_effects=True, vmem_limit_bytes=40 * 2 ** 20),
        name="reduce_grads",
    )(ga, gb.reshape((4, 2) + gb.shape[1:]), dx.reshape((2, 2) + dx.shape[1:]), sm.reshape((4, 2) + sm.shape[1:]))


def mm(a, b, left, right):
    return lax.dot_general(a, b, (((left,), (right,)), ((), ())), preferred_element_type=f32)


def chunks(total, step, body):
    def run(i, _):
        body(pl.ds(pl.multiple_of(i * step, step), step))
        return 0
    lax.fori_loop(0, total // step, run, 0)


def ffn_kernel(n, r, step, mixed, tokens, cot, vec, big, out, dres, ga, dO, small,
               w_out, w_in, w_outer, stage, fb, gp, xh1, n1b, dh2, dm, du, acc, r1, got, lsem, gsem, send, recv):
    toks, model = tokens.shape
    wide = w_in.shape[0]
    per = n // wide
    z, y, x, c, along, ypeer, xpeer, cpeer = grid_peers()
    wire = Wire(send, recv)
    greet([cpeer])
    h = r // 2
    low = lambda size, side: pl.ds(pl.multiple_of(size * side, 16), size)
    def place(s, side, k):
        if k == 0:
            return w_out.at[s, low(h, side)]
        if k <= wide:
            return w_in.at[k - 1, s, low(h, side)]
        return w_outer.at[s // per, s % per, low(wide * h, side)]
    loads = [[] for _ in range(2 + wide)]
    for k in range(2 + wide):
        span = pl.ds(k * h, h if k <= wide else wide * h)
        for s in range(n):
            slot = wire.slot()
            load = pltpu.make_async_copy(big.at[s, span], place(s, c, k), lsem.at[slot])
            load.start()
            wire.start(slot, big.at[s, span], place(s, c, k), cpeer)
            loads[k].append((load, slot, place(s, 1 - c, k)))

    def ready(k):
        for load, slot, spot in loads[k]:
            load.wait()
            wire.arrived(slot, spot, cpeer)

    stores = []

    pending, swaps = [], []

    def finish():
        k, slot, groups, size, span, way = pending.pop()
        wire.arrived(way, got.at[k].reshape((groups, size, model)), cpeer)
        rows, strip = groups * size, min(size, 96)
        def body(i, _):
            at = i * strip
            mine = pl.ds(pl.multiple_of((at // size * 2 + c) * size + at % size, 16), strip)
            theirs = pl.ds(pl.multiple_of(at, 16), strip)
            stage[slot, mine, :] = (stage[slot, mine, :].astype(f32) + got[k, theirs, :].astype(f32)).astype(bf)
            return 0
        lax.fori_loop(0, rows // strip, body, 0)
        whole = stage.at[slot].reshape((groups, 2 * size, model))
        store = pltpu.make_async_copy(whole.at[:, low(size, c)], span, gsem.at[slot])
        store.start()
        stores.append(store)

    def put(value_rows, groups, span):
        k = len(swaps)
        slot = k % stage.shape[0]
        if k >= stage.shape[0]:
            wire.sent(swaps[k - stage.shape[0]])
            stores[k - stage.shape[0]].wait()
        def body(at):
            stage[slot, at, :] = value_rows(at).astype(bf)
        chunks(model, step, body)
        size = model // groups // 2
        way = wire.slot()
        whole = stage.at[slot].reshape((groups, 2 * size, model))
        swaps.append(wire.start(way, whole.at[:, low(size, 1 - c)], got.at[k].reshape((groups, size, model)), cpeer))
        if pending:
            finish()
        pending.append((k, slot, groups, size, span, way))

    flat = lambda ref: ref.reshape(model, model)
    row = lambda i: vec[i:i + 1, :]
    b_output, b_outer, g1, s1, g2, s2 = [row(i) for i in (2, 3, 4, 5, 6, 7)]
    small[...] = jnp.zeros_like(small)
    ready(0)
    wo = flat(w_out)

    def first(at):
        attn = mm(mixed[:, at], wo[...], 0, 0)
        z = tokens[at, :].astype(f32) + (attn + b_output)
        cen = z - jnp.mean(z, axis=-1, keepdims=True)
        inv = lax.rsqrt(jnp.mean(cen * cen, axis=-1, keepdims=True) + NORM_EPS)
        xh = cen * inv
        norm = xh * g1 + s1
        xh1[at, :] = xh
        n1b[at, :] = norm.astype(bf)
        r1[at, :] = jnp.broadcast_to(inv, (inv.shape[0], 128))
        acc[at, :] = norm + b_outer
    chunks(toks, step, first)
    for j in range(wide):
        ready(1 + j)
        wi = flat(w_in.at[j])
        bias = row(8 + j)
        def inner(at, j=j, wi=wi, bias=bias):
            u = mm(n1b[at, :], wi[...], 1, 0) + bias
            cdf = 0.5 * (1.0 + lax.erf(u * (0.5 ** 0.5)))
            pdf = jnp.exp(-0.5 * u * u) * 0.3989422804014327
            fb[j, at, :] = (u * cdf).astype(bf)
            gp[j, at, :] = cdf + u * pdf
        chunks(toks, step, inner)
    ready(1 + wide)
    for j in range(wide):
        wout = flat(w_outer.at[j])
        def outer(at, j=j, wout=wout):
            acc[at, :] += mm(fb[j, at, :], wout[...], 1, 0)
        chunks(toks, step, outer)

    def second(at):
        z = acc[at, :]
        cen = z - jnp.mean(z, axis=-1, keepdims=True)
        inv = lax.rsqrt(jnp.mean(cen * cen, axis=-1, keepdims=True) + NORM_EPS)
        xh = cen * inv
        out[at, :] = (xh * g2 + s2).astype(bf)
        g = cot[at, :].astype(f32)
        gx = g * xh
        gh = g * g2
        d = inv * (gh - jnp.mean(gh, axis=-1, keepdims=True) - xh * jnp.mean(gh * xh, axis=-1, keepdims=True))
        dh2[at, :] = d
        low = d.astype(bf)
        dm[at, :] = low
        small[6:7, :] += jnp.sum(gx, axis=0, keepdims=True)
        small[7:8, :] += jnp.sum(g, axis=0, keepdims=True)
        small[3:4, :] += jnp.sum(low.astype(f32), axis=0, keepdims=True)
    chunks(toks, step, second)
    for j in range(wide):
        wout = flat(w_outer.at[j])
        put(lambda at, j=j: mm(fb[j, :, at], dm[...], 0, 0), per, ga.at[pl.ds(j * per, per), pl.ds((1 + wide) * h, wide * h)])
        def dinner(at, j=j, wout=wout):
            low = (gp[j, at, :] * mm(dm[at, :], wout[...], 1, 1)).astype(bf)
            du[at, :] = low
            small[8 + j:9 + j, :] += jnp.sum(low.astype(f32), axis=0, keepdims=True)
        chunks(toks, step, dinner)
        wi = flat(w_in.at[j])
        def dfirst(at, wi=wi):
            dh2[at, :] += mm(du[at, :], wi[...], 1, 1)
        chunks(toks, step, dfirst)
        put(lambda at: mm(n1b[:, at], du[...], 0, 0), n, ga.at[:, pl.ds((1 + j) * h, h)])

    def last(at):
        d = dh2[at, :]
        xh = xh1[at, :]
        gh = d * g1
        inv = r1[at, 0:1]
        z = inv * (gh - jnp.mean(gh, axis=-1, keepdims=True) - xh * jnp.mean(gh * xh, axis=-1, keepdims=True))
        dres[at, :] = z
        low = z.astype(bf)
        dm[at, :] = low
        small[4:5, :] += jnp.sum(d * xh, axis=0, keepdims=True)
        small[5:6, :] += jnp.sum(d, axis=0, keepdims=True)
        small[2:3, :] += jnp.sum(low.astype(f32), axis=0, keepdims=True)
    chunks(toks, step, last)

    def back(at):
        dO[at, :] = mm(wo[at, :], dm[...], 1, 1).astype(bf)
    chunks(model, step, back)
    put(lambda at: mm(mixed[at, :], dm[...], 1, 0), n, ga.at[:, pl.ds(0, h)])
    finish()
    for store in stores[-stage.shape[0]:]:
        store.wait()
    wire.drain()


def ffn_block(mixed, tokens, cot, vec, big, step=384):
    n, half, model = big.shape
    r = model // n
    wide = (2 * half // r - 1) // 2
    toks = tokens.shape[0]
    vmem = pl.BlockSpec(memory_space=pltpu.VMEM)
    hbm = pl.BlockSpec(memory_space=pl.ANY)
    per = n // wide
    ohold = (per, wide * r, model) if per else (n, r, model)
    V = pltpu.VMEM
    sq = lambda dt, *lead: V(lead + (toks, model), dt)
    return pl.pallas_call(
        functools.partial(ffn_kernel, n, r, step),
        in_specs=[vmem] * 4 + [hbm],
        out_specs=[vmem, vmem, hbm, vmem, vmem],
        out_shape=[jax.ShapeDtypeStruct((toks, model), bf), jax.ShapeDtypeStruct((toks, model), f32),
                   jax.ShapeDtypeStruct((n, half, model), bf), jax.ShapeDtypeStruct((model, toks), bf),
                   jax.ShapeDtypeStruct((16, model), f32)],
        scratch_shapes=[V((n, r, model), bf), V((wide, n, r, model), bf), V((wide,) + ohold, bf), V((4, model, model), bf),
                        sq(bf, wide), sq(f32, wide), sq(f32), sq(bf), sq(f32), sq(bf), sq(bf), sq(f32),
                        V((toks, 128), f32), V((1 + 2 * wide, model // 2, model), bf), pltpu.SemaphoreType.DMA(((2 + wide) * n,)), pltpu.SemaphoreType.DMA((4,)),
                        pltpu.SemaphoreType.DMA(((2 + wide) * n + 1 + 2 * wide,)), pltpu.SemaphoreType.DMA(((2 + wide) * n + 1 + 2 * wide,))],
        compiler_params=pltpu.CompilerParams(collective_id=3, has_side_effects=True, vmem_limit_bytes=67043328),
        cost_estimate=pl.CostEstimate(flops=2 * toks * model * model * (3 + 6 * wide), bytes_accessed=8 * n * half * model, transcendentals=2 * toks * model * wide),
        name="ffn_block",
    )(mixed, tokens, cot, vec, big)


def layer_norm(inputs, norm_gain, norm_bias):
    row_mean = jnp.mean(inputs, axis=-1, keepdims=True)
    centred = inputs - row_mean
    row_var = jnp.mean(centred * centred, axis=-1, keepdims=True)
    return centred * lax.rsqrt(row_var + NORM_EPS) * norm_gain + norm_bias


def gelu_exact(inputs):
    return jax.nn.gelu(inputs, approximate=False)


def contract(left_in, right_in, left_dim, right_dim):
    return lax.dot_general(
        left_in,
        right_in,
        (((left_dim,), (right_dim,)), ((), ())),
        preferred_element_type=jnp.float32,
    )


def chips_of_two_by_four():
    return lax.axis_size("wshard") == 8 and lax.axis_size("seq") == 4


def reduce_parts(ga, gb, dx, sm):
    def scatter(part):
        return lax.psum_scatter(part, "wshard", scatter_dimension=0, tiled=False)

    if chips_of_two_by_four():
        return reduce_grads(scatter(ga), gb, dx, sm)

    fx = lax.psum_scatter(dx, "seq", scatter_dimension=0, tiled=False)
    return (
        lax.psum(scatter(ga), "seq")[None], lax.all_gather(scatter(gb), "seq"), fx, jnp.zeros_like(fx),
        lax.psum(scatter(sm), "seq"),
    )


def ffn_plain(mixed, tokens, cotangent, vec, big):
    shards_n, rows9, model = big.shape
    rows = model // shards_n
    wide = (rows9 // rows - 1) // 2
    bias_output, bias_outer, gain_one, shift_one, gain_two, shift_two = vec[2:8]
    bias_inner = vec[8:8 + wide].reshape(-1)
    output_full = big[:, :rows].reshape(model, model)
    inner_full = jnp.concatenate(
        [big[:, (1 + j) * rows:(2 + j) * rows].reshape(model, model) for j in range(wide)], axis=1
    )
    outer_full = big[:, (1 + wide) * rows:].reshape(-1, model)

    residual_in = tokens.astype(f32) + contract(mixed, output_full, 0, 0) + bias_output
    first_norm, first_back = jax.vjp(layer_norm, residual_in, gain_one, shift_one)
    first_low = first_norm.astype(bf)
    inner_act = jnp.dot(first_low, inner_full, preferred_element_type=f32) + bias_inner
    gelu_out, gelu_back = jax.vjp(gelu_exact, inner_act)
    gelu_low = gelu_out.astype(bf)
    second_in = first_norm + jnp.dot(gelu_low, outer_full, preferred_element_type=f32) + bias_outer
    layer_result, second_back = jax.vjp(layer_norm, second_in, gain_two, shift_two)
    d_second, grad_gain_two, grad_bias_two = second_back(cotangent.astype(f32))
    d_outer = d_second.astype(bf)
    grad_bias_outer = jnp.sum(d_outer.astype(f32), axis=0)
    grad_outer = contract(gelu_low, d_outer, 0, 0)
    (d_inner,) = gelu_back(contract(d_outer, outer_full, 1, 1))
    d_inner_low = d_inner.astype(bf)
    grad_bias_inner = jnp.sum(d_inner_low.astype(f32), axis=0)
    grad_inner = contract(first_low, d_inner_low, 0, 0)
    d_first = contract(d_inner_low, inner_full, 1, 1) + d_second
    d_resid, grad_gain_one, grad_bias_one = first_back(d_first)
    d_attn = d_resid.astype(bf)
    grad_bias_output = jnp.sum(d_attn.astype(f32), axis=0)
    grad_output = contract(mixed, d_attn, 1, 0)
    d_mixed = contract(output_full, d_attn, 1, 1).astype(bf)
    by_rows = lambda grad: grad.astype(bf).reshape(shards_n, -1, model)
    ga = jnp.concatenate(
        [by_rows(grad_output)] + [by_rows(grad_inner[:, j * model:(j + 1) * model]) for j in range(wide)]
        + [by_rows(grad_outer)], axis=1,
    )
    none = jnp.zeros((model,), f32)
    sums = jnp.concatenate([
        jnp.stack([none, none, grad_bias_output, grad_bias_outer, grad_gain_one, grad_bias_one, grad_gain_two, grad_bias_two]),
        grad_bias_inner.reshape(wide, model)], axis=0)
    return layer_result.astype(bf), d_resid, ga, d_mixed, sums


def shards(
    tokens, cotangent, starts,
    w_query, w_key, w_value, w_output, w_inner, w_outer,
    b_query, b_value, b_output, b_inner, b_outer,
    gain_first, bias_first, gain_second, bias_second,
):
    model = tokens.shape[1]
    rows = w_query.shape[0]
    shards_n = lax.axis_size("wshard")
    seq_n = lax.axis_size("seq")
    seq_i = lax.axis_index("seq")
    width = model // seq_n
    heads = width // HD
    wide = w_inner.shape[1] // model

    def own(columns):
        return lax.select_n(seq_i, *jnp.split(columns, seq_n, axis=columns.ndim - 1))

    smalls = (b_query, b_value, b_output, b_outer, gain_first, bias_first, gain_second, bias_second)
    small_cols = jnp.stack(smalls + tuple(b_inner.reshape(wide, rows)), axis=1)
    cols_n = small_cols.shape[1]
    b = jnp.concatenate([own(w_query), own(w_key), own(w_value), jnp.pad(small_cols, ((0, 0), (0, HD - cols_n)))], axis=1)
    fast = chips_of_two_by_four()

    def packed(share, part):
        cut = lambda w: lax.select_n(part == 1, *jnp.split(w, 2)) if share == 2 else w
        inner = cut(w_inner).reshape(rows // share, wide, model).transpose(1, 0, 2).reshape(-1, model)
        return jnp.concatenate([cut(w_output), inner, cut(w_outer)], axis=0)

    if fast:
        big = lax.all_gather(packed(2, seq_i % 2), "wshard")
        side, stream = gather_inputs(b, tokens)
    else:
        big = lax.all_gather(packed(1, 0), "wshard")
        side, stream = lax.all_gather(b, "wshard"), lax.all_gather(tokens, "seq")
    stream = stream.reshape(-1, model)
    side = side.reshape(model, -1)
    w_own = side[:, :3 * width]
    vectors = side[:, 3 * width:3 * width + cols_n].astype(f32).T
    bias_query, bias_value = vectors[:2]
    bias_inner = vectors[8:].reshape(wide, shards_n, rows).transpose(1, 0, 2).reshape(-1)
    scale = HD ** -0.5
    none = jnp.zeros((width,), f32)
    bias = jnp.concatenate([own(bias_query), none, own(bias_value)])
    factor = jnp.where(jnp.arange(3 * width) < width, scale, 1.0)
    qkv = ((contract(w_own, stream, 0, 1) + bias[:, None]) * factor[:, None]).astype(bf)
    oT, mix, lse = attn_fwd(starts, qkv, tokens.shape[0], 512, 512)
    mixed = lax.all_to_all(mix, "seq", split_axis=0, concat_axis=0).reshape(model, -1)

    vec = jnp.concatenate([vectors[:8], bias_inner.reshape(wide, model), jnp.zeros((4, model), f32)], axis=0)
    if fast:
        layer_result, d_resid, ga, d_mixed, sums = ffn_block(mixed, tokens, cotangent, vec, big)
    else:
        layer_result, d_resid, ga, d_mixed, sums = ffn_plain(mixed, tokens, cotangent, vec, big)
    doT = lax.all_to_all(d_mixed.reshape(seq_n, width, -1), "seq", split_axis=0, concat_axis=0)

    dT = attn_bwd(starts, qkv, doT, oT, lse, 256, 512)
    gb = contract(stream, dT, 0, 1).astype(bf).reshape(shards_n, rows, -1)
    dx = contract(dT, w_own, 0, 1).astype(bf).reshape(seq_n, -1, model)
    def spread(own_sum):
        return lax.dynamic_update_slice(jnp.zeros((model,), f32), own_sum, (seq_i * width,))

    d_bias = jnp.sum(dT.astype(f32), axis=1)
    small_rows = (
        spread(d_bias[:width]),
        spread(d_bias[2 * width:]),
        *sums[2:8],
    )
    sm = jnp.concatenate(
        [jnp.stack([row.reshape(shards_n, rows) for row in small_rows], axis=1),
         sums[8:8 + wide].reshape(shards_n, wide, rows)], axis=1,
    )
    sm = jnp.pad(sm, ((0, 0), (0, -cols_n % 8), (0, -rows % 128)))
    fa, fb, fx, fr, fs = reduce_parts(ga, gb, dx, sm)
    d_tokens = fx.astype(f32) + fr.astype(f32) + d_resid
    fb = fb.astype(f32)
    grads = [
        jnp.concatenate([fb[s, :, i * width:(i + 1) * width] for s in range(seq_n)], axis=1) for i in range(3)
    ]
    fa = fa.astype(f32)
    part = rows // fa.shape[0]
    span = lambda first, count: fa[:, first * part:(first + count) * part].reshape(-1, model)
    g_inner = jnp.concatenate([span(1 + j, 1) for j in range(wide)], axis=1)
    tail = [fs[i, :rows] for i in range(8)]
    g_b_inner = fs[8:8 + wide, :rows].reshape(-1)
    return (
        layer_result, d_tokens, *grads,
        span(0, 1), g_inner, span(1 + wide, wide),
        tail[0], tail[1], tail[2], g_b_inner, *tail[3:],
    )


def solution(mesh):
    placed = (
        P(("wshard", "seq"), None),
        P(("wshard", "seq"), None),
        P("wshard", None),
        P("wshard", None),
        P("wshard", None),
        P("wshard", None),
        P("wshard", None),
        P("wshard", None),
        P("wshard", None),
        P("wshard"),
        P("wshard"),
        P("wshard"),
        P("wshard"),
        P("wshard"),
        P("wshard"),
        P("wshard"),
        P("wshard"),
        P("wshard"),
    )
    return jax.shard_map(
        shards,
        mesh=mesh,
        in_specs=placed,
        out_specs=(
            P(("wshard", "seq"), None),
            P(("wshard", "seq"), None),
            P("wshard", None),
            P("wshard", None),
            P("wshard", None),
            P("wshard", None),
            P("wshard", None),
            P("wshard", None),
            P("wshard"),
            P("wshard"),
            P("wshard"),
            P("wshard"),
            P("wshard"),
            P("wshard"),
            P("wshard"),
            P("wshard"),
            P("wshard"),
        ),
        check_vma=False,
    )
```

profile of v0, /device:TPU:0, one launch (start us, length us, event | category | flops | bytes accessed | tf_op | source)
XLA Modules:
  0.0 368.6 jit_solution(1044418047806575583)
XLA Ops:
  7.4 1.2 slice_select_fusion.1
  12.0 35.9 %gather_inputs.1 = (bf16[8,96,640]{2,1,0:T(8,128)(2,1)}, bf16[4,768,768]{2,1,0:T(8,128)(2,1)}) custom-call(bf16[96,640]{1,0:T(8,128)(2,1)} %fusion.3.b_ref, bf16[768,768]{1,0:T(8,128)(2,1)} %tokens.1), custom_call_target="tpu_custom_call" | custom-call | tf_op jit(solution)/shard_map/gather_inputs/pallas_call | solution.py:264
  49.3 7.9 %multiply_convert_fusion.qT.kT.vT = bf16[576,3072]{1,0:T(8,128)(2,1)} fusion(bf16[3072,768]{1,0:T(8,128)(2,1)} %bitcast.128, f32[576]{0:T(1024)S(1)} %fusion.4, f32[576]{0:T(1024)S(1)} %pad_maximum_fusion.5, bf16[768,640]{1,0:T(8,128)(2,1)} %bitcast.109), kind=kOutput, calls=%fused_computation.1 | convolution fusion | flops 2723217408 | bytes 9245184 | tf_op jit(solution)/shard_map/dot_general | solution.py:588
  57.3 41.5 %attn_fwd.1 = (f32[192,3072]{1,0:T(8,128)}, bf16[4,192,768]{2,1,0:T(8,128)(2,1)}, f32[3,3072]{1,0:T(4,128)}) custom-call(s32[1,8]{1,0:T(1,128)} %starts.3, bf16[576,3072]{1,0:T(8,128)(2,1)} %multiply_convert_fusion.qT.kT.vT, bf16[576,3072]{1,0:T(8,128)(2,1)} %multiply_convert_fusion.qT.kT.vT, bf16[576,3072]{1,0:T(8,128)(2,1)} %multiply_convert_fusion.qT.kT.vT), custom_call_target="tpu_custom_call" | custom-call | flops 14495514624 | bytes 4718592 | tf_op jit(solution)/shard_map/attn_fwd/pallas_call | solution.py:78
  98.7 4.3 %all-to-all-start = ((bf16[4,192,768]{2,1,0:T(8,128)(2,1)}), bf16[4,192,768]{2,1,0:T(8,128)(2,1)}, u32[]{:S(2)}, u32[]{:S(2)}) async-start(bf16[4,192,768]{2,1,0:T(8,128)(2,1)} %get-tuple-element.34), calls=%async_computation | async-start | bytes 2359296 | tf_op jit(solution)/shard_map/all_to_all | solution.py:707
  104.1 14.9 %all-to-all-done = bf16[4,192,768]{2,1,0:T(8,128)(2,1)} async-done(((bf16[4,192,768]{2,1,0:T(8,128)(2,1)}), bf16[4,192,768]{2,1,0:T(8,128)(2,1)}, u32[]{:S(2)}, u32[]{:S(2)}) %all-to-all-start) | async-done | bytes 1179680 | tf_op jit(solution)/shard_map/all_to_all | solution.py:707
  119.0 68.2 %ffn_block.1 = (bf16[768,768]{1,0:T(8,128)(2,1)}, f32[768,768]{1,0:T(8,128)}, bf16[8,432,768]{2,1,0:T(8,128)(2,1)}, bf16[768,768]{1,0:T(8,128)(2,1)}, f32[16,768]{1,0:T(8,128)}) custom-call(bf16[768,768]{1,0:T(8,128)(2,1)} %bitcast.17.mixed, bf16[768,768]{1,0:T(8,128)(2,1)} %tokens.1, bf16[768,768]{1,0:T(8,128)(2,1)} %cot.1, ...), custom_call_target="tpu_custom_call" | custom-call | flops 24461180928 | bytes 21233664 | tf_op jit(solution)/shard_map/ffn_block/pallas_call | solution.py:559
  187.2 3.7 all-to-all-start.1
  195.0 11.6 %all-to-all-done.1.doT = bf16[4,192,768]{2,1,0:T(8,128)(2,1)S(1)} async-done(((bf16[4,192,768]{2,1,0:T(8,128)(2,1)}), bf16[4,192,768]{2,1,0:T(8,128)(2,1)S(1)}, u32[]{:S(2)}, u32[]{:S(2)}) %all-to-all-start.1) | async-done | bytes 1179680 | tf_op jit(solution)/shard_map/all_to_all | solution.py:714
  207.7 44.2 %attn_bwd.1 = bf16[576,3072]{1,0:T(8,128)(2,1)} custom-call(s32[1,8]{1,0:T(1,128)} %starts.3, bf16[576,3072]{1,0:T(8,128)(2,1)} %multiply_convert_fusion.qT.kT.vT, bf16[576,3072]{1,0:T(8,128)(2,1)} %multiply_convert_fusion.qT.kT.vT, bf16[576,3072]{1,0:T(8,128)(2,1)} %multiply_convert_fusion.qT.kT.vT, bf16[4,192,768]{2,1,0:T(8,128)(2,1)} %copy-done.5, ...), custom_call_target="tpu_custom_call" | custom-call | flops 14495514624 | bytes 4718592 | tf_op jit(solution)/shard_map/attn_bwd/pallas_call | solution.py:146
  251.9 2.8 convert_reduce_fusion
  255.3 1.4 slice_dynamic-update-slice_fusion.1
  256.7 1.4 stack_reshape.6
  258.6 1.4 slice_dynamic-update-slice_fusion
  260.0 1.4 stack_reshape.7
  261.3 6.1 %convolution_convert_fusion.1 = bf16[768,576]{0,1:T(8,128)(2,1)} fusion(bf16[576,3072]{1,0:T(8,128)(2,1)S(1)} %copy-done.2, bf16[3072,768]{1,0:T(8,128)(2,1)} %bitcast.129), kind=kOutput, calls=%fused_computation.4 | convolution fusion | flops 2718351360 | bytes 9142272 | tf_op jit(solution)/shard_map/dot_general | solution.py:588
  267.5 1.5 copy.83
  269.9 8.4 %convolution_convert_fusion = bf16[3072,768]{1,0:T(8,128)(2,1)} fusion(bf16[576,3072]{1,0:T(8,128)(2,1)} %attn_bwd.1, bf16[768,640]{1,0:T(8,128)(2,1)} %bitcast.110), kind=kOutput, calls=%fused_computation.2 | convolution fusion | flops 2720268288 | bytes 9240576 | tf_op jit(solution)/shard_map/dot_general | solution.py:588
  278.3 19.3 %reduce-scatter.2.cloned.1.call-done = bf16[1,432,768]{2,1,0:T(8,128)(2,1)} async-done(((bf16[8,432,768]{2,1,0:T(8,128)(2,1)}), bf16[1,432,768]{2,1,0:T(8,128)(2,1)}) %reduce-scatter.2.cloned.1.call-update) | async-done | bytes 663568 | tf_op jit(solution)/shard_map/reduce_scatter | solution.py:602
  297.7 2.3 copy-done
  301.1 48.0 %reduce_grads.1 = (bf16[2,432,768]{2,1,0:T(8,128)(2,1)S(1)}, bf16[4,96,576]{2,1,0:T(8,128)(2,1)S(1)}, bf16[768,768]{1,0:T(8,128)(2,1)S(1)}, bf16[768,768]{1,0:T(8,128)(2,1)S(1)}, f32[16,128]{1,0:T(8,128)S(1)}) custom-call(bf16[432,768]{1,0:T(8,128)(2,1)S(1)} %bitcast.97, bf16[4,2,96,576]{3,2,1,0:T(8,128)(2,1)S(1)} %bitcast.96, ...), custom_call_target="tpu_custom_call" | custom-call | tf_op jit(solution)/shard_map/reduce_grads/pallas_call | solution.py:363
  350.0 1.1 slice.187
  353.4 3.4 add_add_fusion
  356.9 1.1 pad_maximum_fusion
  (112 shorter events, 20.8 us)
Async XLA Ops:
  7.2 2.5 copy-start.18
  7.2 3.5 copy-start.21
  7.2 3.6 copy-start.22
  7.2 3.5 copy-start.23
  7.2 3.5 copy-start.24
  7.2 3.5 copy-start.25
  7.3 3.5 copy-start.26
  7.3 3.5 copy-start.27
  7.3 3.5 copy-start.28
  7.3 3.5 copy-start.29
  7.3 3.7 %copy-start.17 = (bf16[96,768]{1,0:T(8,128)(2,1)S(1)}, bf16[96,768]{1,0:T(8,128)(2,1)}, u32[]{:S(2)}) copy-start(bf16[96,768]{1,0:T(8,128)(2,1)} %param.21) | copy-start | bytes 442372
  7.3 111.7 %all-gather.3.cloned.1.call-start = ((), (), s32[]{:S(2)}) async-start(), calls=%async_computation.4 | async-start | bytes 5971968 | tf_op jit(solution)/shard_map/all_gather | solution.py:690
  7.4 3.8 %copy-start.15 = (bf16[96,768]{1,0:T(8,128)(2,1)S(1)}, bf16[96,768]{1,0:T(8,128)(2,1)}, u32[]{:S(2)}) copy-start(bf16[96,768]{1,0:T(8,128)(2,1)} %param.23) | copy-start | bytes 442372
  7.4 3.8 %copy-start.16 = (bf16[96,768]{1,0:T(8,128)(2,1)S(1)}, bf16[96,768]{1,0:T(8,128)(2,1)}, u32[]{:S(2)}) copy-start(bf16[96,768]{1,0:T(8,128)(2,1)} %param.22) | copy-start | bytes 442372
  98.7 20.2 %all-to-all-start = ((bf16[4,192,768]{2,1,0:T(8,128)(2,1)}), bf16[4,192,768]{2,1,0:T(8,128)(2,1)}, u32[]{:S(2)}, u32[]{:S(2)}) async-start(bf16[4,192,768]{2,1,0:T(8,128)(2,1)} %get-tuple-element.34), calls=%async_computation | async-start | bytes 2359296 | tf_op jit(solution)/shard_map/all_to_all | solution.py:707
  103.1 194.6 %reduce-scatter.2.cloned.1.call-start = ((), (), s32[]{:S(2)}) async-start(), calls=%async_computation.3 | async-start | bytes 5971968 | tf_op jit(solution)/shard_map/reduce_scatter | solution.py:602
  187.2 3.7 %copy-start.19 = (f32[16,768]{1,0:T(8,128)S(1)}, f32[16,768]{1,0:T(8,128)}, u32[]{:S(2)}) copy-start(f32[16,768]{1,0:T(8,128)} %get-tuple-element.40) | copy-start | bytes 147460
  187.2 19.5 %all-to-all-start.1 = ((bf16[4,192,768]{2,1,0:T(8,128)(2,1)}), bf16[4,192,768]{2,1,0:T(8,128)(2,1)S(1)}, u32[]{:S(2)}, u32[]{:S(2)}) async-start(bf16[4,192,768]{2,1,0:T(8,128)(2,1)} %bitcast.23), calls=%async_computation.2 | async-start | bytes 2359296 | tf_op jit(solution)/shard_map/all_to_all | solution.py:714
  251.9 9.4 %copy-start.2 = (bf16[576,3072]{1,0:T(8,128)(2,1)S(1)}, bf16[576,3072]{1,0:T(8,128)(2,1)}, u32[]{:S(2)}) copy-start(bf16[576,3072]{1,0:T(8,128)(2,1)} %attn_bwd.1) | copy-start | bytes 10616836
  297.7 2.3 copy-start
  353.4 3.5 copy-start.3
  356.8 2.1 copy-start.7
  356.9 2.9 copy-start.6
  356.9 3.7 %copy-start.4 = (bf16[768,768]{1,0:T(8,128)(2,1)S(1)}, bf16[768,768]{1,0:T(8,128)(2,1)}, u32[]{:S(2)}) copy-start(bf16[768,768]{1,0:T(8,128)(2,1)} %get-tuple-element.103) | copy-start | bytes 3538948
  (10 other events, 13.6 us)
Sparse Core Ops, SparseCore 0:
  10.9 94.6 all-gather.2
  187.3 110.2 reduce-scatter.1
where the time goes:
time: 368 us; the launch traced here: 369 us
  Pallas kernels  238 us (65%)
  waiting for transfers between devices  45.9 us (12%)
  local copies, waits for them, and re-layouts  24.6 us (7%)
  matrix products  22.5 us (6%)
  other arithmetic  15 us (4%)
  between operations  14.7 us (4%)
  starting transfers between devices  8.06 us (2%)
    pallas_call x1, Pallas kernels, ffn_block(): pl.pallas_call(functools.partial(ffn_kernel, n, r, step), in_specs=[vmem]...  68.2 us
    pallas_call x1, Pallas kernels, reduce_grads(): pl.pallas_call(reduce_kernel, in_specs=[vmem] * 4, out_specs=[vmem] * 5,...  48 us
    pallas_call x1, Pallas kernels, attn_bwd(): pl.pallas_call(functools.partial(bwd_kernel, heads, bq, bk), grid=(total...  44.2 us
    pallas_call x1, Pallas kernels, attn_fwd(): pl.pallas_call(functools.partial(fwd_kernel, heads, bq, bk), grid=(total...  41.5 us
    pallas_call x1, Pallas kernels, gather_inputs(): pl.pallas_call(gather_kernel, in_specs=[vmem] * 2, out_specs=[hbm] * 2, o...  35.9 us
    dot_general x3, matrix products, contract(): lax.dot_general(left_in, right_in, (((left_dim,), (right_dim,)), ((), ())...  22.5 us
    reduce_scatter x1, waiting for transfers between devices, scatter(): return lax.psum_scatter(part, 'wshard', scatter_dimension=0, tiled=False)  19.3 us
    all_to_all x1, waiting for transfers between devices, shards(): lax.all_to_all(mix, 'seq', split_axis=0, concat_axis=0).reshape(model, -1)  14.9 us
  transfers between devices with their start and end apart: 4, of which 3 were waited for; matrix products, arithmetic and copies ran while one was open for 11% of the time, Pallas kernels for 33%

commit v1 on v0

--- a/solution.py
+++ b/solution.py
@@ -285,25 +285,35 @@
 ALL = ORDER + (0,)
 
 
-def reduce_kernel(ga, gb, dx, sm, fa, fb, fx, fr, fs, hb, ryb, rzb, rxc, hs, rys, rzs, s1, s2, s3, s4, rg, send, recv):
+def reduce_kernel(ga, gb, dx, sm, fa, fb, fx, fr, fs, hb, ryb, rzb, rxc, hs, rys, rzs, s1, s2, s3, s4, rg, gv, send, recv, lsem):
     z, y, x, c, along, ypeer, xpeer, cpeer = grid_peers()
     wire = Wire(send, recv)
     new = lambda count: [wire.slot() for _ in range(count)]
     kc, kx, kg, kyb, kys = new(4), new(2), new(2), wire.slot(), wire.slot()
-    kzb, kzs, fin = new(4), new(4), new(8)
+    kzb, kzs, fin, kq = new(4), new(4), new(8), new(3)
     zz = lambda d: (z + d) % 4
     half = dx.shape[2] // 2
     halves = [pl.ds(0, half), pl.ds(half, half)]
-    sizes = [ga.shape[0] // 32 * 16, ga.shape[0] - ga.shape[0] // 32 * 16]
+    both = rg.shape[0]
+    quarter = ga.shape[0] - both
+    sizes = [both // 32 * 16, both - both // 32 * 16]
     pieces = [pl.ds(0, sizes[0]), pl.ds(sizes[0], sizes[1])]
+    last = pl.ds(both, quarter)
+    kept = lambda side: pl.ds(pl.multiple_of(both + quarter * side, 16), quarter)
+    fetch = pltpu.make_async_copy(ga.at[pl.ds(0, both)], gv, lsem.at[0])
+    keep = pltpu.make_async_copy(ga.at[last], fa.at[c, kept(x)], lsem.at[1])
+    fetch.start()
+    keep.start()
     greet(along[1:] + [ypeer, xpeer, cpeer])
     for i, at in enumerate(halves):
         wire.start(kc[i], dx.at[1 - x, 1 - c, at], rxc.at[1 - x, at], cpeer)
     wire.start(kg[0], ga.at[pieces[0]], rg.at[pieces[0]], xpeer)
+    wire.start(kq[0], ga.at[last], fa.at[c, kept(x)], xpeer)
     wire.start(kys, sm.at[:, 1 - y], rys, ypeer)
     wire.start(kyb, gb.at[:, 1 - y], ryb, ypeer)
     for i, at in enumerate(halves):
         wire.start(kc[2 + i], dx.at[x, 1 - c, at], rxc.at[x, at], cpeer)
+    wire.start(kq[1], ga.at[last], fa.at[c, kept(x)], cpeer)
     for i, at in enumerate(halves):
         spot = rxc.at[1 - x, at]
         wire.arrived(kc[i], spot, cpeer)
@@ -321,9 +331,12 @@
     for i, at in enumerate(halves):
         wire.arrived(kc[2 + i], rxc.at[x, at], cpeer)
         add_rows(fx.at[at], [dx.at[x, c, at], rxc.at[x, at]], half)
+    fetch.wait()
     wire.arrived(kg[0], rg.at[pieces[0]], xpeer)
-    add_rows(fa.at[c, pieces[0]], [ga.at[pieces[0]], rg.at[pieces[0]]], sizes[0])
+    add_rows(fa.at[c, pieces[0]], [gv.at[pieces[0]], rg.at[pieces[0]]], sizes[0])
     wire.start(fin[5], fa.at[c, pieces[0]], fa.at[c, pieces[0]], cpeer)
+    wire.arrived(kq[0], fa.at[c, kept(1 - x)], xpeer)
+    wire.start(kq[2], fa.at[c, kept(1 - x)], fa.at[c, kept(1 - x)], cpeer)
     for d in ORDER:
         wire.arrived(kzs[d], rzs.at[d], along[d])
         wire.arrived(kzb[d], rzb.at[d], along[d])
@@ -336,7 +349,7 @@
     for i, at in enumerate(halves):
         wire.arrived(kx[i], fr.at[at], xpeer)
     wire.arrived(kg[1], rg.at[pieces[1]], xpeer)
-    add_rows(fa.at[c, pieces[1]], [ga.at[pieces[1]], rg.at[pieces[1]]], sizes[1])
+    add_rows(fa.at[c, pieces[1]], [gv.at[pieces[1]], rg.at[pieces[1]]], sizes[1])
     wire.start(fin[6], fa.at[c, pieces[1]], fa.at[c, pieces[1]], cpeer)
     wire.arrived(fin[0], s2, xpeer)
     s3[...] = s1[...] + s2[...]
@@ -349,26 +362,31 @@
     wire.arrived(fin[4], fb.at[2 * (1 - x) + 1 - c], cpeer)
     for i in range(2):
         wire.arrived(fin[5 + i], fa.at[1 - c, pieces[i]], cpeer)
+    wire.arrived(kq[1], fa.at[1 - c, kept(x)], cpeer)
+    wire.arrived(kq[2], fa.at[1 - c, kept(1 - x)], cpeer)
+    keep.wait()
     wire.drain()
 
 
-def reduce_grads(ga, gb, dx, sm):
-    rows, cols = ga.shape
+def reduce_grads(ga, gb, dx, sm, quarter):
+    both, cols = ga.shape[0] - quarter, ga.shape[1]
+    rows = both + 2 * quarter
     toks = dx.shape[1]
     vmem = pl.BlockSpec(memory_space=pltpu.VMEM)
     b0, b1 = gb.shape[1:]
     V = pltpu.VMEM
     sv = lambda *lead: V(lead + sm.shape[1:], f32)
-    slots = 26
+    slots = 29
     return pl.pallas_call(
         reduce_kernel,
-        in_specs=[vmem] * 4, out_specs=[vmem] * 5,
+        in_specs=[pl.BlockSpec(memory_space=pl.ANY)] + [vmem] * 3, out_specs=[vmem] * 5,
         out_shape=[jax.ShapeDtypeStruct((2, rows, cols), bf), jax.ShapeDtypeStruct((4, b0, b1), bf),
                    jax.ShapeDtypeStruct((toks, cols), bf), jax.ShapeDtypeStruct((toks, cols), bf),
                    jax.ShapeDtypeStruct(sm.shape[1:], f32)],
         scratch_shapes=[V((4, b0, b1), bf), V((4, b0, b1), bf), V((4, b0, b1), bf), V((2, toks, cols), bf),
-                        sv(4), sv(4), sv(4), sv(), sv(), sv(), sv(), V((rows, cols), bf),
-                        pltpu.SemaphoreType.DMA((slots,)), pltpu.SemaphoreType.DMA((slots,))],
+                        sv(4), sv(4), sv(4), sv(), sv(), sv(), sv(), V((both, cols), bf), V((both, cols), bf),
+                        pltpu.SemaphoreType.DMA((slots,)), pltpu.SemaphoreType.DMA((slots,)),
+                        pltpu.SemaphoreType.DMA((2,))],
         compiler_params=pltpu.CompilerParams(collective_id=2, has_side_effects=True, vmem_limit_bytes=40 * 2 ** 20),
         name="reduce_grads",
     )(ga, gb.reshape((4, 2) + gb.shape[1:]), dx.reshape((2, 2) + dx.shape[1:]), sm.reshape((4, 2) + sm.shape[1:]))
@@ -386,13 +404,13 @@
 
 
 def ffn_kernel(n, r, step, mixed, tokens, cot, vec, big, out, dres, ga, dO, small,
-               w_out, w_in, w_outer, stage, fb, gp, xh1, n1b, dh2, dm, du, acc, r1, got, lsem, gsem, send, recv):
+               w_out, w_in, w_outer, stage, fb, gp, xh1, n1b, dh2, dm, du, acc, r1, got, mid, far, lsem, gsem, send, recv):
     toks, model = tokens.shape
     wide = w_in.shape[0]
     per = n // wide
     z, y, x, c, along, ypeer, xpeer, cpeer = grid_peers()
     wire = Wire(send, recv)
-    greet([cpeer])
+    greet([cpeer, xpeer])
     h = r // 2
     low = lambda size, side: pl.ds(pl.multiple_of(size * side, 16), size)
     def place(s, side, k):
@@ -416,32 +434,55 @@
             load.wait()
             wire.arrived(slot, spot, cpeer)
 
-    stores = []
-
-    pending, swaps = [], []
+    stores = {}
+
+    pending, swaps, crossing = [], [], []
+    q = wide * h // 2
+    pair = lambda ref: ref.reshape((per, 2 * q, model))
 
     def finish():
         k, slot, groups, size, span, way = pending.pop()
         wire.arrived(way, got.at[k].reshape((groups, size, model)), cpeer)
-        rows, strip = groups * size, min(size, 96)
+        strip = min(size, r)
+        across = len(crossing) if groups == per else None
         def body(i, _):
             at = i * strip
             mine = pl.ds(pl.multiple_of((at // size * 2 + c) * size + at % size, 16), strip)
             theirs = pl.ds(pl.multiple_of(at, 16), strip)
-            stage[slot, mine, :] = (stage[slot, mine, :].astype(f32) + got[k, theirs, :].astype(f32)).astype(bf)
+            total = (stage[slot, mine, :].astype(f32) + got[k, theirs, :].astype(f32)).astype(bf)
+            if across is None:
+                stage[slot, mine, :] = total
+            else:
+                mid[across, theirs, :] = total
             return 0
-        lax.fori_loop(0, rows // strip, body, 0)
-        whole = stage.at[slot].reshape((groups, 2 * size, model))
-        store = pltpu.make_async_copy(whole.at[:, low(size, c)], span, gsem.at[slot])
+        lax.fori_loop(0, groups * size // strip, body, 0)
+        if across is None:
+            whole = stage.at[slot].reshape((groups, 2 * size, model))
+            store = pltpu.make_async_copy(whole.at[:, low(size, c)], span, gsem.at[slot])
+            store.start()
+            stores[k] = store
+        else:
+            way = wire.slot()
+            wire.start(way, pair(mid.at[across]).at[:, low(q, 1 - x)], far.at[across].reshape((per, q, model)), xpeer)
+            crossing.append((way, span))
+
+    def join(j):
+        way, span = crossing[j]
+        wire.arrived(way, far.at[j].reshape((per, q, model)), xpeer)
+        for g in range(per):
+            mine = pl.ds(pl.multiple_of(g * 2 * q + x * q, 16), q)
+            mid[j, mine, :] = (mid[j, mine, :].astype(f32) + far[j, g * q:(g + 1) * q, :].astype(f32)).astype(bf)
+        store = pltpu.make_async_copy(pair(mid.at[j]).at[:, low(q, x)], span, gsem.at[stage.shape[0] + j])
         store.start()
-        stores.append(store)
+        return store
 
     def put(value_rows, groups, span):
         k = len(swaps)
         slot = k % stage.shape[0]
         if k >= stage.shape[0]:
             wire.sent(swaps[k - stage.shape[0]])
-            stores[k - stage.shape[0]].wait()
+            if k - stage.shape[0] in stores:
+                stores.pop(k - stage.shape[0]).wait()
         def body(at):
             stage[slot, at, :] = value_rows(at).astype(bf)
         chunks(model, step, body)
@@ -509,7 +550,7 @@
     chunks(toks, step, second)
     for j in range(wide):
         wout = flat(w_outer.at[j])
-        put(lambda at, j=j: mm(fb[j, :, at], dm[...], 0, 0), per, ga.at[pl.ds(j * per, per), pl.ds((1 + wide) * h, wide * h)])
+        put(lambda at, j=j: mm(fb[j, :, at], dm[...], 0, 0), per, ga.at[pl.ds(j * per, per), pl.ds((1 + wide) * h, q)])
         def dinner(at, j=j, wout=wout):
             low = (gp[j, at, :] * mm(dm[at, :], wout[...], 1, 1)).astype(bf)
             du[at, :] = low
@@ -540,7 +581,8 @@
     chunks(model, step, back)
     put(lambda at: mm(mixed[at, :], dm[...], 1, 0), n, ga.at[:, pl.ds(0, h)])
     finish()
-    for store in stores[-stage.shape[0]:]:
+    joined = [join(j) for j in range(wide)]
+    for store in [*stores.values(), *joined]:
         store.wait()
     wire.drain()
 
@@ -561,12 +603,13 @@
         in_specs=[vmem] * 4 + [hbm],
         out_specs=[vmem, vmem, hbm, vmem, vmem],
         out_shape=[jax.ShapeDtypeStruct((toks, model), bf), jax.ShapeDtypeStruct((toks, model), f32),
-                   jax.ShapeDtypeStruct((n, half, model), bf), jax.ShapeDtypeStruct((model, toks), bf),
+                   jax.ShapeDtypeStruct((n, half - wide * r // 4, model), bf), jax.ShapeDtypeStruct((model, toks), bf),
                    jax.ShapeDtypeStruct((16, model), f32)],
         scratch_shapes=[V((n, r, model), bf), V((wide, n, r, model), bf), V((wide,) + ohold, bf), V((4, model, model), bf),
                         sq(bf, wide), sq(f32, wide), sq(f32), sq(bf), sq(f32), sq(bf), sq(bf), sq(f32),
-                        V((toks, 128), f32), V((1 + 2 * wide, model // 2, model), bf), pltpu.SemaphoreType.DMA(((2 + wide) * n,)), pltpu.SemaphoreType.DMA((4,)),
-                        pltpu.SemaphoreType.DMA(((2 + wide) * n + 1 + 2 * wide,)), pltpu.SemaphoreType.DMA(((2 + wide) * n + 1 + 2 * wide,))],
+                        V((toks, 128), f32), V((1 + 2 * wide, model // 2, model), bf),
+                        V((wide, model // 2, model), bf), V((wide, model // 4, model), bf), pltpu.SemaphoreType.DMA(((2 + wide) * n,)), pltpu.SemaphoreType.DMA((4 + wide,)),
+                        pltpu.SemaphoreType.DMA(((2 + wide) * n + 1 + 3 * wide,)), pltpu.SemaphoreType.DMA(((2 + wide) * n + 1 + 3 * wide,))],
         compiler_params=pltpu.CompilerParams(collective_id=3, has_side_effects=True, vmem_limit_bytes=67043328),
         cost_estimate=pl.CostEstimate(flops=2 * toks * model * model * (3 + 6 * wide), bytes_accessed=8 * n * half * model, transcendentals=2 * toks * model * wide),
         name="ffn_block",
@@ -597,12 +640,12 @@
     return lax.axis_size("wshard") == 8 and lax.axis_size("seq") == 4
 
 
-def reduce_parts(ga, gb, dx, sm):
+def reduce_parts(ga, gb, dx, sm, quarter):
     def scatter(part):
         return lax.psum_scatter(part, "wshard", scatter_dimension=0, tiled=False)
 
     if chips_of_two_by_four():
-        return reduce_grads(scatter(ga), gb, dx, sm)
+        return reduce_grads(scatter(ga), gb, dx, sm, quarter)
 
     fx = lax.psum_scatter(dx, "seq", scatter_dimension=0, tiled=False)
     return (
@@ -653,7 +696,7 @@
     none = jnp.zeros((model,), f32)
     sums = jnp.concatenate([
         jnp.stack([none, none, grad_bias_output, grad_bias_outer, grad_gain_one, grad_bias_one, grad_gain_two, grad_bias_two]),
-        grad_bias_inner.reshape(wide, model)], axis=0)
+        grad_bias_inner.reshape(wide, model), jnp.zeros((4, model), f32)], axis=0)
     return layer_result.astype(bf), d_resid, ga, d_mixed, sums
 
 
@@ -716,21 +759,16 @@
     dT = attn_bwd(starts, qkv, doT, oT, lse, 256, 512)
     gb = contract(stream, dT, 0, 1).astype(bf).reshape(shards_n, rows, -1)
     dx = contract(dT, w_own, 0, 1).astype(bf).reshape(seq_n, -1, model)
-    def spread(own_sum):
-        return lax.dynamic_update_slice(jnp.zeros((model,), f32), own_sum, (seq_i * width,))
-
-    d_bias = jnp.sum(dT.astype(f32), axis=1)
-    small_rows = (
-        spread(d_bias[:width]),
-        spread(d_bias[2 * width:]),
-        *sums[2:8],
-    )
+    d_bias = contract(jnp.ones((8, dT.shape[1]), bf), dT, 1, 1)[:1]
+    column = lax.broadcasted_iota(jnp.int32, (1, model), 1)
+    spread = lambda own_sum: jnp.where(column // width == seq_i, jnp.tile(own_sum, (1, seq_n)), 0.0)
+    row = lax.broadcasted_iota(jnp.int32, (sums.shape[0], 1), 0)
+    sums = jnp.where(row == 0, spread(d_bias[:, :width]), jnp.where(row == 1, spread(d_bias[:, 2 * width:]), sums))
     sm = jnp.concatenate(
-        [jnp.stack([row.reshape(shards_n, rows) for row in small_rows], axis=1),
-         sums[8:8 + wide].reshape(shards_n, wide, rows)], axis=1,
+        [sums[:8].reshape(8, shards_n, rows).transpose(1, 0, 2), sums[8:8 + wide].reshape(shards_n, wide, rows)], axis=1,
     )
     sm = jnp.pad(sm, ((0, 0), (0, -cols_n % 8), (0, -rows % 128)))
-    fa, fb, fx, fr, fs = reduce_parts(ga, gb, dx, sm)
+    fa, fb, fx, fr, fs = reduce_parts(ga, gb, dx, sm, wide * rows // 4)
     d_tokens = fx.astype(f32) + fr.astype(f32) + d_resid
     fb = fb.astype(f32)
     grads = [

time: 368 us -> 363 us (0.986); the launches traced: 369 us -> 359 us
  waiting for transfers between devices: 45.9 us -> 36 us
  local copies, waits for them, and re-layouts: 24.6 us -> 18 us
  Pallas kernels: 238 us -> 242 us
    reduce_scatter x1, waiting for transfers between devices: 19.3 us -> 5.82 us  [scatter(): return lax.psum_scatter(part, 'wshard', scatter_dimension=0, tiled=False)]
    another operation x11 -> x4, local copies, waits for them, and re-layouts: 7.94 us -> 0.17 us  [shards(): jnp.tile(own_sum, (1, seq_n))]
    pallas_call x1, Pallas kernels: 68.2 us -> 72 us  [ffn_block(): pl.pallas_call(functools.partial(ffn_kernel, n, r, step), in_specs=[vmem]...]
    dot_general x3 -> x4, matrix products: 22.5 us -> 25.6 us  [contract(): lax.dot_general(left_in, right_in, (((left_dim,), (right_dim,)), ((), ())...]
where the time goes in v1:
time: 363 us; the launch traced here: 359 us
  Pallas kernels  242 us (67%)
  waiting for transfers between devices  36 us (10%)
  matrix products  25.6 us (7%)
  local copies, waits for them, and re-layouts  18 us (5%)
  between operations  14.7 us (4%)
  other arithmetic  14.4 us (4%)
  starting transfers between devices  7.9 us (2%)
    pallas_call x1, Pallas kernels, ffn_block(): pl.pallas_call(functools.partial(ffn_kernel, n, r, step), in_specs=[vmem]...  72 us
    pallas_call x1, Pallas kernels, reduce_grads(): pl.pallas_call(reduce_kernel, in_specs=[pl.BlockSpec(memory_space=pl.ANY)...  51.2 us
    pallas_call x1, Pallas kernels, attn_bwd(): pl.pallas_call(functools.partial(bwd_kernel, heads, bq, bk), grid=(total...  41.9 us
    pallas_call x1, Pallas kernels, attn_fwd(): pl.pallas_call(functools.partial(fwd_kernel, heads, bq, bk), grid=(total...  41.5 us
    pallas_call x1, Pallas kernels, gather_inputs(): pl.pallas_call(gather_kernel, in_specs=[vmem] * 2, out_specs=[hbm] * 2, o...  35.9 us
    dot_general x4, matrix products, contract(): lax.dot_general(left_in, right_in, (((left_dim,), (right_dim,)), ((), ())...  25.6 us
    all_to_all x1, waiting for transfers between devices, shards(): lax.all_to_all(d_mixed.reshape(seq_n, width, -1), 'seq', split_axis=0, co...  15.3 us
    all_to_all x1, waiting for transfers between devices, shards(): lax.all_to_all(mix, 'seq', split_axis=0, concat_axis=0).reshape(model, -1)  14.9 us
  transfers between devices with their start and end apart: 4, of which 3 were waited for; matrix products, arithmetic and copies ran while one was open for 11% of the time, Pallas kernels for 33%

profile of v1, /device:TPU:0, one launch (start us, length us, event | category | flops | bytes accessed | tf_op | source)
XLA Modules:
  0.0 359.1 jit_solution(1529377366804669935)
XLA Ops:
  7.4 1.2 slice_select_fusion.1
  8.6 1.1 slice_select_fusion
  12.1 35.9 %gather_inputs.1 = (bf16[8,96,640]{2,1,0:T(8,128)(2,1)}, bf16[4,768,768]{2,1,0:T(8,128)(2,1)}) custom-call(bf16[96,640]{1,0:T(8,128)(2,1)} %fusion.3.b_ref, bf16[768,768]{1,0:T(8,128)(2,1)} %tokens.1), custom_call_target="tpu_custom_call" | custom-call | tf_op jit(solution)/shard_map/gather_inputs/pallas_call | solution.py:264
  49.4 7.9 %multiply_convert_fusion.qT.kT.vT = bf16[576,3072]{1,0:T(8,128)(2,1)} fusion(bf16[3072,768]{1,0:T(8,128)(2,1)} %bitcast.125, f32[576]{0:T(1024)S(1)} %fusion.9, f32[576]{0:T(1024)S(1)} %pad_maximum_fusion.5, bf16[768,640]{1,0:T(8,128)(2,1)} %bitcast.110), kind=kOutput, calls=%fused_computation | convolution fusion | flops 2723217408 | bytes 9245184 | tf_op jit(solution)/shard_map/dot_general | solution.py:631
  57.3 41.5 %attn_fwd.1 = (f32[192,3072]{1,0:T(8,128)}, bf16[4,192,768]{2,1,0:T(8,128)(2,1)}, f32[3,3072]{1,0:T(4,128)}) custom-call(s32[1,8]{1,0:T(1,128)} %starts.3, bf16[576,3072]{1,0:T(8,128)(2,1)} %multiply_convert_fusion.qT.kT.vT, bf16[576,3072]{1,0:T(8,128)(2,1)} %multiply_convert_fusion.qT.kT.vT, bf16[576,3072]{1,0:T(8,128)(2,1)} %multiply_convert_fusion.qT.kT.vT), custom_call_target="tpu_custom_call" | custom-call | flops 14495514624 | bytes 4718592 | tf_op jit(solution)/shard_map/attn_fwd/pallas_call | solution.py:78
  98.8 4.3 %all-to-all-start = ((bf16[4,192,768]{2,1,0:T(8,128)(2,1)}), bf16[4,192,768]{2,1,0:T(8,128)(2,1)}, u32[]{:S(2)}, u32[]{:S(2)}) async-start(bf16[4,192,768]{2,1,0:T(8,128)(2,1)} %get-tuple-element.34), calls=%async_computation | async-start | bytes 2359296 | tf_op jit(solution)/shard_map/all_to_all | solution.py:750
  104.1 14.9 %all-to-all-done = bf16[4,192,768]{2,1,0:T(8,128)(2,1)} async-done(((bf16[4,192,768]{2,1,0:T(8,128)(2,1)}), bf16[4,192,768]{2,1,0:T(8,128)(2,1)}, u32[]{:S(2)}, u32[]{:S(2)}) %all-to-all-start) | async-done | bytes 1179680 | tf_op jit(solution)/shard_map/all_to_all | solution.py:750
  119.0 72.0 %ffn_block.1 = (bf16[768,768]{1,0:T(8,128)(2,1)}, f32[768,768]{1,0:T(8,128)}, bf16[8,336,768]{2,1,0:T(8,128)(2,1)}, bf16[768,768]{1,0:T(8,128)(2,1)}, f32[16,768]{1,0:T(8,128)}) custom-call(bf16[768,768]{1,0:T(8,128)(2,1)} %bitcast.17.mixed, bf16[768,768]{1,0:T(8,128)(2,1)} %tokens.1, bf16[768,768]{1,0:T(8,128)(2,1)} %cot.1, ...), custom_call_target="tpu_custom_call" | custom-call | flops 24461180928 | bytes 21233664 | tf_op jit(solution)/shard_map/ffn_block/pallas_call | solution.py:601
  191.0 3.5 all-to-all-start.1
  195.1 15.3 %all-to-all-done.1.doT = bf16[4,192,768]{2,1,0:T(8,128)(2,1)S(1)} async-done(((bf16[4,192,768]{2,1,0:T(8,128)(2,1)}), bf16[4,192,768]{2,1,0:T(8,128)(2,1)S(1)}, u32[]{:S(2)}, u32[]{:S(2)}) %all-to-all-start.1) | async-done | bytes 1179680 | tf_op jit(solution)/shard_map/all_to_all | solution.py:757
  211.4 41.9 %attn_bwd.1 = bf16[576,3072]{1,0:T(8,128)(2,1)} custom-call(s32[1,8]{1,0:T(1,128)} %starts.3, bf16[576,3072]{1,0:T(8,128)(2,1)} %multiply_convert_fusion.qT.kT.vT, bf16[576,3072]{1,0:T(8,128)(2,1)} %multiply_convert_fusion.qT.kT.vT, bf16[576,3072]{1,0:T(8,128)(2,1)} %multiply_convert_fusion.qT.kT.vT, bf16[4,192,768]{2,1,0:T(8,128)(2,1)} %copy-done.4, ...), custom_call_target="tpu_custom_call" | custom-call | flops 14495514624 | bytes 4718592 | tf_op jit(solution)/shard_map/attn_bwd/pallas_call | solution.py:146
  253.3 3.2 fusion.4
  258.7 1.4 reshape.189
  260.2 1.4 copy.81
  262.3 6.2 %convolution_convert_fusion.1 = bf16[768,576]{0,1:T(8,128)(2,1)} fusion(bf16[576,3072]{1,0:T(8,128)(2,1)S(1)} %copy-done.2, bf16[3072,768]{1,0:T(8,128)(2,1)} %bitcast.126), kind=kOutput, calls=%fused_computation.3 | convolution fusion | flops 2718351360 | bytes 9142272 | tf_op jit(solution)/shard_map/dot_general | solution.py:631
  268.5 1.5 copy.73
  270.8 8.4 %convolution_convert_fusion = bf16[3072,768]{1,0:T(8,128)(2,1)} fusion(bf16[576,3072]{1,0:T(8,128)(2,1)} %attn_bwd.1, bf16[768,640]{1,0:T(8,128)(2,1)} %bitcast.111), kind=kOutput, calls=%fused_computation.1 | convolution fusion | flops 2720268288 | bytes 9240576 | tf_op jit(solution)/shard_map/dot_general | solution.py:631
  279.2 5.8 %reduce-scatter.2.cloned.1.call-done = bf16[1,336,768]{2,1,0:T(8,128)(2,1)} async-done(((bf16[8,336,768]{2,1,0:T(8,128)(2,1)}), bf16[1,336,768]{2,1,0:T(8,128)(2,1)}) %reduce-scatter.2.cloned.1.call-update) | async-done | bytes 516112 | tf_op jit(solution)/shard_map/reduce_scatter | solution.py:645
  285.0 2.3 copy-done
  288.4 51.2 %reduce_grads.1 = (bf16[2,432,768]{2,1,0:T(8,128)(2,1)S(1)}, bf16[4,96,576]{2,1,0:T(8,128)(2,1)S(1)}, bf16[768,768]{1,0:T(8,128)(2,1)S(1)}, bf16[768,768]{1,0:T(8,128)(2,1)S(1)}, f32[16,128]{1,0:T(8,128)S(1)}) custom-call(bf16[336,768]{1,0:T(8,128)(2,1)S(1)} %bitcast.97, bf16[4,2,96,576]{3,2,1,0:T(8,128)(2,1)S(1)} %bitcast.96, ...), custom_call_target="tpu_custom_call" | custom-call | tf_op jit(solution)/shard_map/reduce_grads/pallas_call | solution.py:380
  340.4 1.1 slice.191
  342.2 1.1 slice_bitcast_fusion.3
  343.9 3.4 add_add_fusion
  347.4 1.1 pad_maximum_fusion
  (110 shorter events, 16.8 us)
Async XLA Ops:
  7.2 2.5 copy-start.20
  7.2 3.5 copy-start.21
  7.2 3.6 copy-start.22
  7.2 3.5 copy-start.23
  7.2 3.5 copy-start.24
  7.2 3.5 copy-start.25
  7.3 3.5 copy-start.26
  7.3 3.5 copy-start.27
  7.3 3.5 copy-start.28
  7.3 3.5 copy-start.29
  7.3 3.7 %copy-start.17 = (bf16[96,768]{1,0:T(8,128)(2,1)S(1)}, bf16[96,768]{1,0:T(8,128)(2,1)}, u32[]{:S(2)}) copy-start(bf16[96,768]{1,0:T(8,128)(2,1)} %param.23) | copy-start | bytes 442372
  7.3 111.7 %all-gather.3.cloned.1.call-start = ((), (), s32[]{:S(2)}) async-start(), calls=%async_computation.4 | async-start | bytes 5971968 | tf_op jit(solution)/shard_map/all_gather | solution.py:733
  7.4 3.8 %copy-start.18 = (bf16[96,768]{1,0:T(8,128)(2,1)S(1)}, bf16[96,768]{1,0:T(8,128)(2,1)}, u32[]{:S(2)}) copy-start(bf16[96,768]{1,0:T(8,128)(2,1)} %param.22) | copy-start | bytes 442372
  7.4 3.9 %copy-start.19 = (bf16[96,768]{1,0:T(8,128)(2,1)S(1)}, bf16[96,768]{1,0:T(8,128)(2,1)}, u32[]{:S(2)}) copy-start(bf16[96,768]{1,0:T(8,128)(2,1)} %param.21) | copy-start | bytes 442372
  98.8 20.2 %all-to-all-start = ((bf16[4,192,768]{2,1,0:T(8,128)(2,1)}), bf16[4,192,768]{2,1,0:T(8,128)(2,1)}, u32[]{:S(2)}, u32[]{:S(2)}) async-start(bf16[4,192,768]{2,1,0:T(8,128)(2,1)} %get-tuple-element.34), calls=%async_computation | async-start | bytes 2359296 | tf_op jit(solution)/shard_map/all_to_all | solution.py:750
  103.1 182.0 %reduce-scatter.2.cloned.1.call-start = ((), (), s32[]{:S(2)}) async-start(), calls=%async_computation.3 | async-start | bytes 4644864 | tf_op jit(solution)/shard_map/reduce_scatter | solution.py:645
  191.0 19.3 %all-to-all-start.1 = ((bf16[4,192,768]{2,1,0:T(8,128)(2,1)}), bf16[4,192,768]{2,1,0:T(8,128)(2,1)S(1)}, u32[]{:S(2)}, u32[]{:S(2)}) async-start(bf16[4,192,768]{2,1,0:T(8,128)(2,1)} %bitcast.23), calls=%async_computation.2 | async-start | bytes 2359296 | tf_op jit(solution)/shard_map/all_to_all | solution.py:757
  253.3 9.1 %copy-start.2 = (bf16[576,3072]{1,0:T(8,128)(2,1)S(1)}, bf16[576,3072]{1,0:T(8,128)(2,1)}, u32[]{:S(2)}) copy-start(bf16[576,3072]{1,0:T(8,128)(2,1)} %attn_bwd.1) | copy-start | bytes 10616836
  285.0 2.3 copy-start
  347.3 2.9 copy-start.5
  347.3 2.9 copy-start.6
  347.3 2.9 copy-start.7
  347.3 2.9 copy-start.8
  347.4 3.7 %copy-start.3 = (bf16[768,768]{1,0:T(8,128)(2,1)S(1)}, bf16[768,768]{1,0:T(8,128)(2,1)}, u32[]{:S(2)}) copy-start(bf16[768,768]{1,0:T(8,128)(2,1)} %get-tuple-element.101) | copy-start | bytes 3538948
  (10 other events, 15.2 us)
Sparse Core Ops, SparseCore 0:
  10.9 94.6 all-gather.2
  191.2 93.8 reduce-scatter.1

commit v2 on v1

--- a/solution.py
+++ b/solution.py
@@ -760,14 +760,18 @@
     gb = contract(stream, dT, 0, 1).astype(bf).reshape(shards_n, rows, -1)
     dx = contract(dT, w_own, 0, 1).astype(bf).reshape(seq_n, -1, model)
     d_bias = contract(jnp.ones((8, dT.shape[1]), bf), dT, 1, 1)[:1]
-    column = lax.broadcasted_iota(jnp.int32, (1, model), 1)
-    spread = lambda own_sum: jnp.where(column // width == seq_i, jnp.tile(own_sum, (1, seq_n)), 0.0)
-    row = lax.broadcasted_iota(jnp.int32, (sums.shape[0], 1), 0)
-    sums = jnp.where(row == 0, spread(d_bias[:, :width]), jnp.where(row == 1, spread(d_bias[:, 2 * width:]), sums))
     sm = jnp.concatenate(
         [sums[:8].reshape(8, shards_n, rows).transpose(1, 0, 2), sums[8:8 + wide].reshape(shards_n, wide, rows)], axis=1,
     )
-    sm = jnp.pad(sm, ((0, 0), (0, -cols_n % 8), (0, -rows % 128)))
+    lanes = -rows % 128
+    sm = jnp.pad(sm, ((0, 0), (0, -cols_n % 8), (0, lanes)))
+    shard, row = (lax.broadcasted_iota(jnp.int32, sm.shape, axis) for axis in (0, 1))
+    per = width // rows
+    for r, first in ((0, 0), (1, 2 * width)):
+        for t in range(per):
+            at = first + t * rows
+            own_sum = jnp.pad(d_bias[:, at:at + rows], ((0, 0), (0, lanes)))
+            sm = jnp.where((row == r) & (shard == seq_i * per + t), own_sum[None], sm)
     fa, fb, fx, fr, fs = reduce_parts(ga, gb, dx, sm, wide * rows // 4)
     d_tokens = fx.astype(f32) + fr.astype(f32) + d_resid
     fb = fb.astype(f32)

time: 363 us -> 340 us (0.937); the launches traced: 359 us -> 340 us
  Pallas kernels: 242 us -> 225 us
  waiting for transfers between devices: 36 us -> 45.1 us
  local copies, waits for them, and re-layouts: 18 us -> 12.4 us
    pallas_call x1, Pallas kernels: 72 us -> 58.9 us  [ffn_block(): pl.pallas_call(functools.partial(ffn_kernel, n, r, step), in_specs=[vmem]...]
    reduce_scatter x1, waiting for transfers between devices: 5.82 us -> 14.6 us  [scatter(): return lax.psum_scatter(part, 'wshard', scatter_dimension=0, tiled=False)]
    pallas_call x1, Pallas kernels: 51.2 us -> 45.2 us  [reduce_grads(): pl.pallas_call(reduce_kernel, in_specs=[pl.BlockSpec(memory_space=pl.ANY)...]
  transfers between devices with their start and end apart: 4 -> 4, of which waited for: 3 -> 3; matrix products, arithmetic and copies ran while one was open for 11% -> 8% of each run, Pallas kernels for 33% -> 35%
where the time goes in v2:
time: 340 us
  Pallas kernels  225 us (66%)
  waiting for transfers between devices  45.1 us (13%)
  matrix products  23.1 us (7%)
  between operations  14.6 us (4%)
  local copies, waits for them, and re-layouts  12.4 us (4%)
  other arithmetic  12.3 us (4%)
  starting transfers between devices  7.9 us (2%)
    pallas_call x1, Pallas kernels, ffn_block(): pl.pallas_call(functools.partial(ffn_kernel, n, r, step), in_specs=[vmem]...  58.9 us
    pallas_call x1, Pallas kernels, reduce_grads(): pl.pallas_call(reduce_kernel, in_specs=[pl.BlockSpec(memory_space=pl.ANY)...  45.2 us
    pallas_call x1, Pallas kernels, attn_bwd(): pl.pallas_call(functools.partial(bwd_kernel, heads, bq, bk), grid=(total...  43 us
    pallas_call x1, Pallas kernels, attn_fwd(): pl.pallas_call(functools.partial(fwd_kernel, heads, bq, bk), grid=(total...  41.5 us
    pallas_call x1, Pallas kernels, gather_inputs(): pl.pallas_call(gather_kernel, in_specs=[vmem] * 2, out_specs=[hbm] * 2, o...  35.9 us
    dot_general x4, matrix products, contract(): lax.dot_general(left_in, right_in, (((left_dim,), (right_dim,)), ((), ())...  23.1 us
    all_to_all x1, waiting for transfers between devices, shards(): lax.all_to_all(d_mixed.reshape(seq_n, width, -1), 'seq', split_axis=0, co...  15.5 us
    all_to_all x1, waiting for transfers between devices, shards(): lax.all_to_all(mix, 'seq', split_axis=0, concat_axis=0).reshape(model, -1)  14.9 us
  transfers between devices with their start and end apart: 4, of which 3 were waited for; matrix products, arithmetic and copies ran while one was open for 8% of the time, Pallas kernels for 35%

profile of v2, /device:TPU:0, one launch (start us, length us, event | category | flops | bytes accessed | tf_op | source)
XLA Modules:
  0.0 339.9 jit_solution(11260316921705452975)
XLA Ops:
  7.4 1.2 slice_select_fusion.1
  8.6 1.1 slice_select_fusion
  12.0 35.9 %gather_inputs.1 = (bf16[8,96,640]{2,1,0:T(8,128)(2,1)}, bf16[4,768,768]{2,1,0:T(8,128)(2,1)}) custom-call(bf16[96,640]{1,0:T(8,128)(2,1)} %fusion.3.b_ref, bf16[768,768]{1,0:T(8,128)(2,1)} %tokens.1), custom_call_target="tpu_custom_call" | custom-call | tf_op jit(solution)/shard_map/gather_inputs/pallas_call | solution.py:264
  48.0 1.0 slice.177
  49.3 7.9 %multiply_convert_fusion.qT.kT.vT = bf16[576,3072]{1,0:T(8,128)(2,1)} fusion(bf16[3072,768]{1,0:T(8,128)(2,1)} %bitcast.129, f32[576]{0:T(1024)S(1)} %fusion.10, f32[576]{0:T(1024)S(1)} %pad_maximum_fusion.5, bf16[768,640]{1,0:T(8,128)(2,1)} %bitcast.116), kind=kOutput, calls=%fused_computation | convolution fusion | flops 2723217408 | bytes 9245184 | tf_op jit(solution)/shard_map/dot_general | solution.py:631
  57.2 41.5 %attn_fwd.1 = (f32[192,3072]{1,0:T(8,128)}, bf16[4,192,768]{2,1,0:T(8,128)(2,1)}, f32[3,3072]{1,0:T(4,128)}) custom-call(s32[1,8]{1,0:T(1,128)} %starts.3, bf16[576,3072]{1,0:T(8,128)(2,1)} %multiply_convert_fusion.qT.kT.vT, bf16[576,3072]{1,0:T(8,128)(2,1)} %multiply_convert_fusion.qT.kT.vT, bf16[576,3072]{1,0:T(8,128)(2,1)} %multiply_convert_fusion.qT.kT.vT), custom_call_target="tpu_custom_call" | custom-call | flops 14495514624 | bytes 4718592 | tf_op jit(solution)/shard_map/attn_fwd/pallas_call | solution.py:78
  98.7 4.3 %all-to-all-start = ((bf16[4,192,768]{2,1,0:T(8,128)(2,1)}), bf16[4,192,768]{2,1,0:T(8,128)(2,1)}, u32[]{:S(2)}, u32[]{:S(2)}) async-start(bf16[4,192,768]{2,1,0:T(8,128)(2,1)} %get-tuple-element.34), calls=%async_computation | async-start | bytes 2359296 | tf_op jit(solution)/shard_map/all_to_all | solution.py:750
  104.0 14.9 %all-to-all-done = bf16[4,192,768]{2,1,0:T(8,128)(2,1)} async-done(((bf16[4,192,768]{2,1,0:T(8,128)(2,1)}), bf16[4,192,768]{2,1,0:T(8,128)(2,1)}, u32[]{:S(2)}, u32[]{:S(2)}) %all-to-all-start) | async-done | bytes 1179680 | tf_op jit(solution)/shard_map/all_to_all | solution.py:750
  118.9 58.9 %ffn_block.1 = (bf16[768,768]{1,0:T(8,128)(2,1)}, f32[768,768]{1,0:T(8,128)}, bf16[8,336,768]{2,1,0:T(8,128)(2,1)}, bf16[768,768]{1,0:T(8,128)(2,1)}, f32[16,768]{1,0:T(8,128)}) custom-call(bf16[768,768]{1,0:T(8,128)(2,1)} %bitcast.17.mixed, bf16[768,768]{1,0:T(8,128)(2,1)} %tokens.1, bf16[768,768]{1,0:T(8,128)(2,1)} %cot.1, ...), custom_call_target="tpu_custom_call" | custom-call | flops 24461180928 | bytes 21233664 | tf_op jit(solution)/shard_map/ffn_block/pallas_call | solution.py:601
  177.9 3.5 %all-to-all-start.1 = ((bf16[4,192,768]{2,1,0:T(8,128)(2,1)}), bf16[4,192,768]{2,1,0:T(8,128)(2,1)S(1)}, u32[]{:S(2)}, u32[]{:S(2)}) async-start(bf16[4,192,768]{2,1,0:T(8,128)(2,1)} %bitcast.23), calls=%async_computation.2 | async-start | bytes 2359296 | tf_op jit(solution)/shard_map/all_to_all | solution.py:757
  181.7 15.5 %all-to-all-done.1.doT = bf16[4,192,768]{2,1,0:T(8,128)(2,1)S(1)} async-done(((bf16[4,192,768]{2,1,0:T(8,128)(2,1)}), bf16[4,192,768]{2,1,0:T(8,128)(2,1)S(1)}, u32[]{:S(2)}, u32[]{:S(2)}) %all-to-all-start.1) | async-done | bytes 1179680 | tf_op jit(solution)/shard_map/all_to_all | solution.py:757
  197.2 1.0 copy-done.5
  198.2 43.0 %attn_bwd.1 = bf16[576,3072]{1,0:T(8,128)(2,1)} custom-call(s32[1,8]{1,0:T(1,128)} %starts.3, bf16[576,3072]{1,0:T(8,128)(2,1)} %multiply_convert_fusion.qT.kT.vT, bf16[576,3072]{1,0:T(8,128)(2,1)} %multiply_convert_fusion.qT.kT.vT, bf16[576,3072]{1,0:T(8,128)(2,1)} %multiply_convert_fusion.qT.kT.vT, bf16[4,192,768]{2,1,0:T(8,128)(2,1)} %copy-done.5, ...), custom_call_target="tpu_custom_call" | custom-call | flops 14495514624 | bytes 4718592 | tf_op jit(solution)/shard_map/attn_bwd/pallas_call | solution.py:146
  241.2 6.4 %convolution_convert_fusion.1 = bf16[768,576]{0,1:T(8,128)(2,1)S(1)} fusion(bf16[576,3072]{1,0:T(8,128)(2,1)} %attn_bwd.1, bf16[3072,768]{1,0:T(8,128)(2,1)} %bitcast.130), kind=kOutput, calls=%fused_computation.3 | convolution fusion | flops 2718351360 | bytes 9142272 | tf_op jit(solution)/shard_map/dot_general | solution.py:631
  248.3 3.2 fusion.8
  251.7 5.7 %convolution_convert_fusion = bf16[3072,768]{1,0:T(8,128)(2,1)} fusion(bf16[576,3072]{1,0:T(8,128)(2,1)S(1)} %copy-done.2, bf16[768,640]{1,0:T(8,128)(2,1)S(1)} %bitcast.117), kind=kOutput, calls=%fused_computation.1 | convolution fusion | flops 2720268288 | bytes 9240576 | tf_op jit(solution)/shard_map/dot_general | solution.py:631
  257.4 14.6 %reduce-scatter.2.cloned.1.call-done = bf16[1,336,768]{2,1,0:T(8,128)(2,1)} async-done(((bf16[8,336,768]{2,1,0:T(8,128)(2,1)}), bf16[1,336,768]{2,1,0:T(8,128)(2,1)}) %reduce-scatter.2.cloned.1.call-update) | async-done | bytes 516112 | tf_op jit(solution)/shard_map/reduce_scatter | solution.py:645
  272.0 2.3 copy-done
  274.4 1.0 copy-done.1
  275.4 45.2 %reduce_grads.1 = (bf16[2,432,768]{2,1,0:T(8,128)(2,1)S(1)}, bf16[4,96,576]{2,1,0:T(8,128)(2,1)S(1)}, bf16[768,768]{1,0:T(8,128)(2,1)S(1)}, bf16[768,768]{1,0:T(8,128)(2,1)S(1)}, f32[16,128]{1,0:T(8,128)S(1)}) custom-call(bf16[336,768]{1,0:T(8,128)(2,1)S(1)} %bitcast.103, bf16[4,2,96,576]{3,2,1,0:T(8,128)(2,1)S(1)} %bitcast.102, ...), custom_call_target="tpu_custom_call" | custom-call | tf_op jit(solution)/shard_map/reduce_grads/pallas_call | solution.py:380
  321.5 1.1 slice.201
  324.9 3.4 %add_add_fusion = f32[768,768]{1,0:T(8,128)} fusion(f32[768,768]{1,0:T(8,128)} %get-tuple-element.43, bf16[768,768]{1,0:T(8,128)(2,1)S(1)} %get-tuple-element.42, bf16[768,768]{1,0:T(8,128)(2,1)S(1)} %get-tuple-element.41), kind=kLoop, calls=%fused_computation.2 | loop fusion | flops 2359296 | bytes 7077888 | tf_op jit(solution)/shard_map/add | solution.py:776
  328.4 1.1 pad_maximum_fusion
  332.1 1.0 copy.84
  (109 shorter events, 10.4 us)
Async XLA Ops:
  7.2 2.5 copy-start.18
  7.2 3.5 %copy-start.21 = (bf16[384]{0:T(512)(128)(2,1)S(1)}, bf16[384]{0:T(512)(128)(2,1)}, u32[]{:S(2)}) copy-start(bf16[384]{0:T(512)(128)(2,1)} %param.30) | copy-start | bytes 2308
  7.2 3.6 %copy-start.22 = (bf16[96]{0:T(256)(128)(2,1)S(1)}, bf16[96]{0:T(256)(128)(2,1)}, u32[]{:S(2)}) copy-start(bf16[96]{0:T(256)(128)(2,1)} %param.27) | copy-start | bytes 580
  7.2 3.5 %copy-start.23 = (bf16[96]{0:T(256)(128)(2,1)S(1)}, bf16[96]{0:T(256)(128)(2,1)}, u32[]{:S(2)}) copy-start(bf16[96]{0:T(256)(128)(2,1)} %param.28) | copy-start | bytes 580
  7.2 3.5 %copy-start.24 = (bf16[96]{0:T(256)(128)(2,1)S(1)}, bf16[96]{0:T(256)(128)(2,1)}, u32[]{:S(2)}) copy-start(bf16[96]{0:T(256)(128)(2,1)} %param.29) | copy-start | bytes 580
  7.2 3.5 %copy-start.25 = (bf16[96]{0:T(256)(128)(2,1)S(1)}, bf16[96]{0:T(256)(128)(2,1)}, u32[]{:S(2)}) copy-start(bf16[96]{0:T(256)(128)(2,1)} %param.31) | copy-start | bytes 580
  7.3 3.5 %copy-start.26 = (bf16[96]{0:T(256)(128)(2,1)S(1)}, bf16[96]{0:T(256)(128)(2,1)}, u32[]{:S(2)}) copy-start(bf16[96]{0:T(256)(128)(2,1)} %param.32) | copy-start | bytes 580
  7.3 3.5 %copy-start.27 = (bf16[96]{0:T(256)(128)(2,1)S(1)}, bf16[96]{0:T(256)(128)(2,1)}, u32[]{:S(2)}) copy-start(bf16[96]{0:T(256)(128)(2,1)} %param.33) | copy-start | bytes 580
  7.3 3.5 %copy-start.28 = (bf16[96]{0:T(256)(128)(2,1)S(1)}, bf16[96]{0:T(256)(128)(2,1)}, u32[]{:S(2)}) copy-start(bf16[96]{0:T(256)(128)(2,1)} %param.34) | copy-start | bytes 580
  7.3 3.5 %copy-start.29 = (bf16[96]{0:T(256)(128)(2,1)S(1)}, bf16[96]{0:T(256)(128)(2,1)}, u32[]{:S(2)}) copy-start(bf16[96]{0:T(256)(128)(2,1)} %param.35) | copy-start | bytes 580
  7.3 3.7 %copy-start.17 = (bf16[96,768]{1,0:T(8,128)(2,1)S(1)}, bf16[96,768]{1,0:T(8,128)(2,1)}, u32[]{:S(2)}) copy-start(bf16[96,768]{1,0:T(8,128)(2,1)} %param.21) | copy-start | bytes 442372
  7.3 111.6 %all-gather.3.cloned.1.call-start = ((), (), s32[]{:S(2)}) async-start(), calls=%async_computation.4 | async-start | bytes 5971968 | tf_op jit(solution)/shard_map/all_gather | solution.py:733
  7.4 3.8 %copy-start.15 = (bf16[96,768]{1,0:T(8,128)(2,1)S(1)}, bf16[96,768]{1,0:T(8,128)(2,1)}, u32[]{:S(2)}) copy-start(bf16[96,768]{1,0:T(8,128)(2,1)} %param.23) | copy-start | bytes 442372
  7.4 3.8 %copy-start.16 = (bf16[96,768]{1,0:T(8,128)(2,1)S(1)}, bf16[96,768]{1,0:T(8,128)(2,1)}, u32[]{:S(2)}) copy-start(bf16[96,768]{1,0:T(8,128)(2,1)} %param.22) | copy-start | bytes 442372
  98.7 20.2 %all-to-all-start = ((bf16[4,192,768]{2,1,0:T(8,128)(2,1)}), bf16[4,192,768]{2,1,0:T(8,128)(2,1)}, u32[]{:S(2)}, u32[]{:S(2)}) async-start(bf16[4,192,768]{2,1,0:T(8,128)(2,1)} %get-tuple-element.34), calls=%async_computation | async-start | bytes 2359296 | tf_op jit(solution)/shard_map/all_to_all | solution.py:750
  103.0 169.0 %reduce-scatter.2.cloned.1.call-start = ((), (), s32[]{:S(2)}) async-start(), calls=%async_computation.3 | async-start | bytes 4644864 | tf_op jit(solution)/shard_map/reduce_scatter | solution.py:645
  177.8 3.6 %copy-start.20 = (f32[16,768]{1,0:T(8,128)S(1)}, f32[16,768]{1,0:T(8,128)}, u32[]{:S(2)}) copy-start(f32[16,768]{1,0:T(8,128)} %get-tuple-element.40) | copy-start | bytes 147460
  177.9 19.3 %all-to-all-start.1 = ((bf16[4,192,768]{2,1,0:T(8,128)(2,1)}), bf16[4,192,768]{2,1,0:T(8,128)(2,1)S(1)}, u32[]{:S(2)}, u32[]{:S(2)}) async-start(bf16[4,192,768]{2,1,0:T(8,128)(2,1)} %bitcast.23), calls=%async_computation.2 | async-start | bytes 2359296 | tf_op jit(solution)/shard_map/all_to_all | solution.py:757
  247.6 4.1 %copy-start.19 = (bf16[8,96,640]{2,1,0:T(8,128)(2,1)S(1)}, bf16[8,96,640]{2,1,0:T(8,128)(2,1)}, u32[]{:S(2)}) copy-start(bf16[8,96,640]{2,1,0:T(8,128)(2,1)} %get-tuple-element.32) | copy-start | bytes 2949124
  248.3 3.4 %copy-start.2 = (bf16[576,3072]{1,0:T(8,128)(2,1)S(1)}, bf16[576,3072]{1,0:T(8,128)(2,1)}, u32[]{:S(2)}) copy-start(bf16[576,3072]{1,0:T(8,128)(2,1)} %attn_bwd.1) | copy-start | bytes 10616836
  272.0 2.3 copy-start
  324.9 3.5 %copy-start.3 = (f32[2,48,768]{2,1,0:T(8,128)S(1)}, f32[2,48,768]{2,1,0:T(8,128)}, u32[]{:S(2)}) copy-start(f32[2,48,768]{2,1,0:T(8,128)} %get-tuple-element.50) | copy-start | bytes 884740
  328.3 2.9 copy-start.6
  328.4 3.7 %copy-start.4 = (bf16[768,768]{1,0:T(8,128)(2,1)S(1)}, bf16[768,768]{1,0:T(8,128)(2,1)}, u32[]{:S(2)}) copy-start(bf16[768,768]{1,0:T(8,128)(2,1)} %get-tuple-element.103) | copy-start | bytes 3538948
  (10 other events, 15.0 us)
Sparse Core Ops, SparseCore 0:
  10.9 94.7 all-gather.2
  178.0 93.9 reduce-scatter.1
